TPU v7x, 32 devices: a whole 2x2x4 slice. The times are simulated.
32 devices in a mesh: tok: 2 (over y), hid: 16 (over z, x, core).
Axes of the slice: x: 2, y: 2, z: 4, core: 2. Of those that a mesh axis runs over, the one named last changes fastest.
Arguments:
- student_in: bfloat16 [256, 8192], P('hid', 'tok'), may hold values from -6 to 6
- target_delta: bfloat16 [256, 8192], P('hid', 'tok'), may hold values from -3 to 3
- gate_weight: bfloat16 [8192, 16384], P('tok', 'hid'), may hold values from -0.0625 to 0.0625
- up_weight: bfloat16 [8192, 16384], P('tok', 'hid'), may hold values from -0.0625 to 0.0625
- down_weight: bfloat16 [16384, 8192], P('hid', 'tok'), may hold values from -0.046875 to 0.046875
- block_mask: int32 [3, 64, 128], P(None, 'tok', 'hid'), may hold values from 0 to 1, as said below
Outputs:
- student_out: bfloat16 [256, 8192], P('hid', 'tok')
- input_grad: bfloat16 [256, 8192], P('hid', 'tok')
- gate_wgrad: float32 [8192, 16384], P('tok', 'hid')
- up_wgrad: float32 [8192, 16384], P('tok', 'hid')
- down_wgrad: float32 [16384, 8192], P('hid', 'tok')
Inputs may be any that keep to these rules, and one draw needn't show every extreme that they name: `block_mask`: each entry is 0 or 1 (1 keeps a 128 x 128 block of weights); the share of ones differs from one block column of hidden units to another.
All inputs are finite; a program needn't handle non-finite values.
Results may differ from a plain program's by a relative error of at most 0.0056.
Values may be sent and summed in bfloat16 or wider, within the bound.
No kernel may reach another device: no remote copies, remote signals or barrier semaphores. Data moves between devices by JAX's collectives and lax.ppermute only.
A program may use at most 192 MiB of HBM per device.

v0:
```python
import jax
import jax.numpy as jnp
from jax import lax
from jax.sharding import PartitionSpec as P

BLOCK = 128


def widen(blocks):
    return jnp.repeat(jnp.repeat(blocks, BLOCK, axis=0), BLOCK, axis=1)


def per_device(student_in, target_delta, gate_weight, up_weight, down_weight, block_mask):
    by_cols = (((1,), (1,)), ((), ()))
    by_rows = (((0,), (0,)), ((), ()))
    gate_mask = widen(block_mask[0]).astype(jnp.bfloat16)
    up_mask = widen(block_mask[1]).astype(jnp.bfloat16)
    down_mask = widen(block_mask[2]).T.astype(jnp.bfloat16)
    gate_eff = gate_weight * gate_mask
    up_eff = up_weight * up_mask
    down_eff = down_weight * down_mask
    hidden_cols = gate_weight.shape[1]
    rows_end = student_in.shape[0]
    total_rows = rows_end * lax.axis_size("hid")
    factor = 1.0 / jnp.sqrt(jnp.float32(total_rows))
    inputs_all = lax.all_gather(student_in, "hid", axis=0, tiled=True)
    piece = inputs_all
    gate_part = jnp.dot(piece, gate_eff, preferred_element_type=jnp.float32)
    up_part = jnp.dot(piece, up_eff, preferred_element_type=jnp.float32)
    both = lax.psum_scatter(
        jnp.concatenate([gate_part, up_part], axis=1), "tok", scatter_dimension=0, tiled=True
    )
    gate = both[:, :hidden_cols]
    up = both[:, hidden_cols:]
    sigma = jax.nn.sigmoid(gate)
    swish = gate * sigma
    hidden = (swish * up).astype(jnp.bfloat16)
    hidden_all = lax.all_gather(hidden, "tok", axis=0, tiled=True)
    piece = hidden_all
    output_sum = lax.psum_scatter(
        jnp.dot(piece, down_eff, preferred_element_type=jnp.float32),
        "hid",
        scatter_dimension=0,
        tiled=True,
    )
    error = (output_sum - target_delta.astype(jnp.float32)).astype(jnp.bfloat16)
    error_all = lax.all_gather(error, "hid", axis=0, tiled=True)
    piece = error_all
    hidden_grad = lax.psum_scatter(
        lax.dot_general(piece, down_eff, by_cols, preferred_element_type=jnp.float32),
        "tok",
        scatter_dimension=0,
        tiled=True,
    )
    gate_grad = (hidden_grad * up * (sigma + gate * sigma * (1.0 - sigma))).astype(jnp.bfloat16)
    up_grad = (hidden_grad * swish).astype(jnp.bfloat16)
    gate_grad_all, up_grad_all = (
        lax.all_gather(gate_grad, "tok", axis=0, tiled=True),
        lax.all_gather(up_grad, "tok", axis=0, tiled=True),
    )
    gate_wgrad = (
        lax.dot_general(inputs_all, gate_grad_all, by_rows, preferred_element_type=jnp.float32)
        * gate_mask.astype(jnp.float32)
        * factor
    )
    up_wgrad = (
        lax.dot_general(inputs_all, up_grad_all, by_rows, preferred_element_type=jnp.float32)
        * up_mask.astype(jnp.float32)
        * factor
    )
    down_wgrad = (
        lax.dot_general(hidden_all, error_all, by_rows, preferred_element_type=jnp.float32)
        * down_mask.astype(jnp.float32)
        * factor
    )
    first = lax.dot_general(gate_grad_all, gate_eff, by_cols, preferred_element_type=jnp.float32)
    input_grad = lax.psum_scatter(
        first + lax.dot_general(up_grad_all, up_eff, by_cols, preferred_element_type=jnp.float32),
        "hid",
        scatter_dimension=0,
        tiled=True,
    ).astype(jnp.bfloat16)
    return (output_sum.astype(jnp.bfloat16), input_grad, gate_wgrad, up_wgrad, down_wgrad)


def solution(mesh):
    placed = (
        P("hid", "tok"),
        P("hid", "tok"),
        P("tok", "hid"),
        P("tok", "hid"),
        P("hid", "tok"),
        P(None, "tok", "hid"),
    )
    return jax.shard_map(
        per_device,
        mesh=mesh,
        in_specs=placed,
        out_specs=(
            P("hid", "tok"),
            P("hid", "tok"),
            P("tok", "hid"),
            P("tok", "hid"),
            P("hid", "tok"),
        ),
        check_vma=False,
    )
```

profile of v0, /device:TPU:0, one launch (start us, length us, event | category | flops | bytes accessed | tf_op | source)
XLA Modules:
  0.0 367.3 jit_solution(6142179612223112247)
XLA Ops:
  7.2 0.0 all-gather.3.cloned.1.call-start
  7.2 0.7 all-gather.3.cloned.1.call-update
  7.9 0.0 copy-start.5
  7.9 0.0 reduce-scatter.5.cloned.1.call-start
  8.0 11.9 %copy.14 = bf16[4096,1024]{0,1:T(8,128)(2,1)} copy(bf16[4096,1024]{1,0:T(8,128)(2,1)} %param.9) | data formatting | bytes 16777216 | tf_op args[3]
  19.9 0.0 copy-done.5
  19.9 0.1 copy.13
  20.0 11.9 %copy.12 = bf16[4096,1024]{0,1:T(8,128)(2,1)} copy(bf16[4096,1024]{1,0:T(8,128)(2,1)} %param.8) | data formatting | bytes 16777216 | tf_op args[2]
  31.9 0.1 copy.11
  32.0 0.1 broadcast_bitcast_fusion.1
  32.1 7.4 %bitcast_multiply_fusion.3 = bf16[4096,1024]{0,1:T(8,128)(2,1)} fusion(bf16[4096,1024]{0,1:T(8,128)(2,1)} %copy.14, bf16[4096,8]{0,1:T(8,128)(2,1)S(1)} %broadcast_bitcast_fusion.1), kind=kLoop, calls=%fused_computation.6 | loop fusion | flops 4194304 | bytes 16842752 | tf_op jit(solution)/shard_map/mul | solution.py:20
  39.5 0.1 broadcast_bitcast_fusion.2
  39.6 7.4 %bitcast_multiply_fusion.4 = bf16[4096,1024]{0,1:T(8,128)(2,1)} fusion(bf16[4096,1024]{0,1:T(8,128)(2,1)} %copy.12, bf16[4096,8]{0,1:T(8,128)(2,1)S(1)} %broadcast_bitcast_fusion.2), kind=kLoop, calls=%fused_computation.7 | loop fusion | flops 4194304 | bytes 16842752 | tf_op jit(solution)/shard_map/mul | solution.py:19
  47.0 7.4 %all-gather.3.cloned.1.call-done = bf16[256,4096]{1,0:T(8,128)(2,1)} async-done(((bf16[16,4096]{1,0:T(8,128)(2,1)}), bf16[256,4096]{1,0:T(8,128)(2,1)}) %all-gather.3.cloned.1.call-update) | async-done | bytes 2097168 | tf_op jit(solution)/shard_map/all_gather | solution.py:26
  54.3 0.0 copy-start
  54.3 0.0 copy-start.1
  54.3 6.5 %convolution_bitcast_fusion = f32[256,1024]{0,1:T(8,128)S(1)} fusion(bf16[4096,1024]{0,1:T(8,128)(2,1)} %bitcast_multiply_fusion.3, bf16[256,4096]{1,0:T(8,128)(2,1)} %all-gather.3.cloned.1.call-done), kind=kOutput, calls=%fused_computation.10 | convolution fusion | flops 2147483648 | bytes 11534336 | tf_op jit(solution)/shard_map/dot_general | solution.py:29
  60.8 0.0 copy-done
  60.9 0.5 copy-done.1
  61.3 2.4 convolution_bitcast_fusion.1
  63.7 1.5 pad_maximum_fusion
  65.2 0.0 reduce-scatter.5.cloned.1.call-update
  65.2 0.0 reduce-scatter.7.cloned.1.call-start
  65.2 0.1 copy.15
  65.3 0.1 broadcast_bitcast_fusion
  65.4 7.4 %bitcast_multiply_fusion.2 = bf16[1024,4096]{1,0:T(8,128)(2,1)} fusion(bf16[1024,4096]{1,0:T(8,128)(2,1)} %param.10, bf16[4096,8]{0,1:T(8,128)(2,1)S(1)} %broadcast_bitcast_fusion), kind=kLoop, calls=%fused_computation.5 | loop fusion | flops 4194304 | bytes 16842752 | tf_op jit(solution)/shard_map/mul | solution.py:21
  72.8 23.2 %reduce-scatter.5.cloned.1.call-done = f32[128,2048]{0,1:T(8,128)} async-done(((f32[256,2048]{0,1:T(8,128)}), f32[128,2048]{0,1:T(8,128)}) %reduce-scatter.5.cloned.1.call-update) | async-done | bytes 1048592 | tf_op jit(solution)/shard_map/reduce_scatter | solution.py:30
  96.0 1.3 multiply_convert_fusion.2
  97.3 8.6 %all_gather.16 = bf16[256,1024]{0,1:T(8,128)(2,1)S(1)} all-gather(bf16[128,1024]{0,1:T(8,128)(2,1)S(1)} %multiply_convert_fusion.2), channel_id=1, replica_groups=mesh['tok'=2,'hid'=16] {'tok'}, dimensions={0}, use_global_device_ids=true | all-gather | bytes 786432 | tf_op jit(solution)/shard_map/all_gather | solution.py:38
  105.9 0.0 copy-start.4
  105.9 7.8 %fusion.2 = f32[256,4096]{1,0:T(8,128)} fusion(bf16[256,1024]{0,1:T(8,128)(2,1)S(1)} %all_gather.16, bf16[1024,4096]{1,0:T(8,128)(2,1)} %bitcast_multiply_fusion.2), kind=kOutput, calls=%fused_computation.24 | convolution fusion | flops 2147483648 | bytes 13107200 | tf_op jit(solution)/shard_map/dot_general | solution.py:41
  113.7 0.0 reduce-scatter.7.cloned.1.call-update
  113.7 0.0 all-gather.5.cloned.1.call-start
  113.7 72.9 %reduce-scatter.7.cloned.1.call-done = f32[16,4096]{1,0:T(8,128)} async-done(((f32[256,4096]{1,0:T(8,128)}), f32[16,4096]{1,0:T(8,128)}) %reduce-scatter.7.cloned.1.call-update) | async-done | bytes 262160 | tf_op jit(solution)/shard_map/reduce_scatter | solution.py:40
  186.6 0.0 copy-done.4
  186.6 1.8 subtract_convert_fusion
  188.4 0.0 all-gather.5.cloned.1.call-update
  188.4 0.2 reduce-scatter.9.cloned.1.call-start
  188.6 41.1 %all-gather.5.cloned.1.call-done = bf16[256,4096]{1,0:T(8,128)(2,1)} async-done(((bf16[16,4096]{1,0:T(8,128)(2,1)}), bf16[256,4096]{1,0:T(8,128)(2,1)}) %all-gather.5.cloned.1.call-update) | async-done | bytes 2097168 | tf_op jit(solution)/shard_map/all_gather | solution.py:47
  229.7 7.4 %fusion.3 = f32[256,1024]{0,1:T(8,128)} fusion(bf16[256,4096]{1,0:T(8,128)(2,1)} %all-gather.5.cloned.1.call-done, bf16[1024,4096]{1,0:T(8,128)(2,1)} %bitcast_multiply_fusion.2), kind=kOutput, calls=%fused_computation.25 | convolution fusion | flops 2147483648 | bytes 11534336 | tf_op jit(solution)/shard_map/dot_general | solution.py:50
  237.1 0.0 reduce-scatter.9.cloned.1.call-update
  237.1 0.0 reduce-scatter.11.cloned.1.call-start
  237.2 19.2 %reduce-scatter.9.cloned.1.call-done = f32[128,1024]{0,1:T(8,128)} async-done(((f32[256,1024]{0,1:T(8,128)}), f32[128,1024]{0,1:T(8,128)}) %reduce-scatter.9.cloned.1.call-update) | async-done | bytes 524304 | tf_op jit(solution)/shard_map/reduce_scatter | solution.py:49
  256.4 1.6 multiply_convert_fusion
  258.0 0.0 slice-start
  258.0 8.7 %all_gather.18 = bf16[256,1024]{0,1:T(8,128)(2,1)S(1)} all-gather(bf16[128,1024]{0,1:T(8,128)(2,1)S(1)} %get-tuple-element.11), channel_id=1, replica_groups=mesh['tok'=2,'hid'=16] {'tok'}, dimensions={0}, use_global_device_ids=true | all-gather | bytes 786432 | tf_op jit(solution)/shard_map/all_gather | solution.py:58
  266.7 0.0 slice-start.1
  266.7 6.1 %fusion.4 = f32[256,4096]{1,0:T(8,128)S(1)} fusion(bf16[256,1024]{0,1:T(8,128)(2,1)S(1)} %all_gather.18, bf16[4096,1024]{0,1:T(8,128)(2,1)} %bitcast_multiply_fusion.4), kind=kOutput, calls=%fused_computation.26 | convolution fusion | flops 2147483648 | bytes 13107200 | tf_op jit(solution)/shard_map/dot_general | solution.py:76
  272.8 7.7 %all_gather.19 = bf16[256,1024]{0,1:T(8,128)(2,1)S(1)} all-gather(bf16[128,1024]{0,1:T(8,128)(2,1)S(1)} %get-tuple-element.10), channel_id=1, replica_groups=mesh['tok'=2,'hid'=16] {'tok'}, dimensions={0}, use_global_device_ids=true | all-gather | bytes 786432 | tf_op jit(solution)/shard_map/all_gather | solution.py:59
  280.5 0.0 copy-start.2
  280.5 0.8 copy-done.2
  281.3 0.0 slice-done
  281.3 0.0 slice-done.1
  281.3 4.7 %convolution_add_fusion = f32[256,4096]{1,0:T(8,128)} fusion(f32[256,4096]{1,0:T(8,128)S(1)} %fusion.4, bf16[256,1024]{0,1:T(8,128)(2,1)S(1)} %all_gather.19, bf16[4096,1024]{0,1:T(8,128)(2,1)S(1)} %bitcast.54), kind=kOutput, calls=%fused_computation.8 | convolution fusion | flops 2148532224 | bytes 17301504 | tf_op jit(solution)/shard_map/dot_general | solution.py:78
  286.0 0.0 reduce-scatter.11.cloned.1.call-update
  286.0 10.3 %multiply_multiply_fusion = f32[1024,4096]{1,0:T(8,128)} fusion(bf16[256,1024]{0,1:T(8,128)(2,1)S(1)} %all_gather.16, bf16[256,4096]{1,0:T(8,128)(2,1)} %all-gather.5.cloned.1.call-done, bf16[4096,8]{0,1:T(8,128)(2,1)S(1)} %broadcast_bitcast_fusion), kind=kOutput, calls=%fused_computation.4 | convolution fusion | flops 2160066560 | bytes 19464192 | tf_op jit(solution)/shard_map/dot_general | solution.py:72
  296.3 8.9 %fusion.1 = f32[4096,1024]{0,1:T(8,128)} fusion(bf16[256,1024]{0,1:T(8,128)(2,1)S(1)} %all_gather.18, bf16[256,4096]{1,0:T(8,128)(2,1)S(1)} %copy-done.1, bf16[4096,8]{0,1:T(8,128)(2,1)S(1)} %broadcast_bitcast_fusion.2), kind=kOutput, calls=%fused_computation.3 | convolution fusion | flops 2160066560 | bytes 19464192 | tf_op jit(solution)/shard_map/dot_general | solution.py:62
  305.2 0.0 copy-start.3
  305.2 17.6 %copy.17 = f32[4096,1024]{1,0:T(8,128)} copy(f32[4096,1024]{0,1:T(8,128)} %fusion.1) | data formatting | bytes 33554432
  322.8 0.0 copy-done.3
  322.9 8.1 %fusion = f32[4096,1024]{0,1:T(8,128)} fusion(bf16[256,1024]{0,1:T(8,128)(2,1)S(1)} %copy-done.3, bf16[256,4096]{1,0:T(8,128)(2,1)S(1)} %copy-done.1, bf16[4096,8]{0,1:T(8,128)(2,1)S(1)} %broadcast_bitcast_fusion.1), kind=kOutput, calls=%fused_computation.1 | convolution fusion | flops 2160066560 | bytes 19464192 | tf_op jit(solution)/shard_map/dot_general | solution.py:67
  330.9 17.5 %copy.18 = f32[4096,1024]{1,0:T(8,128)} copy(f32[4096,1024]{0,1:T(8,128)} %fusion) | data formatting | bytes 33554432
  348.5 10.4 %reduce-scatter.11.cloned.1.call-done = f32[16,4096]{1,0:T(8,128)} async-done(((f32[256,4096]{1,0:T(8,128)}), f32[16,4096]{1,0:T(8,128)}) %reduce-scatter.11.cloned.1.call-update) | async-done | bytes 262160 | tf_op jit(solution)/shard_map/reduce_scatter | solution.py:77
  358.9 1.6 convert_element_type.85
  (3 shorter events, 0.0 us)
Async XLA Ops:
  7.2 47.2 %all-gather.3.cloned.1.call-start = ((), (), s32[]{:S(2)}) async-start(), calls=%async_computation.4 | async-start | bytes 2228224 | tf_op jit(solution)/shard_map/all_gather | solution.py:26
  7.9 12.0 %copy-start.5 = (s32[3,32,8]{1,2,0:T(8,128)S(1)}, s32[3,32,8]{1,2,0:T(8,128)}, u32[]{:S(2)}) copy-start(s32[3,32,8]{1,2,0:T(8,128)} %param.11) | copy-start | bytes 9220
  7.9 88.1 %reduce-scatter.5.cloned.1.call-start = ((), (), s32[]{:S(2)}) async-start(), calls=%async_computation.5 | async-start | bytes 3145728 | tf_op jit(solution)/shard_map/reduce_scatter | solution.py:30
  54.3 6.5 %copy-start = (bf16[4096,1024]{0,1:T(8,128)(2,1)S(1)}, bf16[4096,1024]{0,1:T(8,128)(2,1)}, u32[]{:S(2)}) copy-start(bf16[4096,1024]{0,1:T(8,128)(2,1)} %bitcast_multiply_fusion.4) | copy-start | bytes 25165828
  54.3 7.0 %copy-start.1 = (bf16[256,4096]{1,0:T(8,128)(2,1)S(1)}, bf16[256,4096]{1,0:T(8,128)(2,1)}, u32[]{:S(2)}) copy-start(bf16[256,4096]{1,0:T(8,128)(2,1)} %all-gather.3.cloned.1.call-done) | copy-start | bytes 6291460
  65.2 121.4 %reduce-scatter.7.cloned.1.call-start = ((), (), s32[]{:S(2)}) async-start(), calls=%async_computation.6 | async-start | bytes 4456448 | tf_op jit(solution)/shard_map/reduce_scatter | solution.py:40
  105.9 80.7 %copy-start.4 = (bf16[16,4096]{1,0:T(8,128)(2,1)S(1)}, bf16[16,4096]{1,0:T(8,128)(2,1)}, u32[]{:S(2)}) copy-start(bf16[16,4096]{1,0:T(8,128)(2,1)} %param.7) | copy-start | bytes 393220
  113.7 116.1 %all-gather.5.cloned.1.call-start = ((), (), s32[]{:S(2)}) async-start(), calls=%async_computation.7 | async-start | bytes 2228224 | tf_op jit(solution)/shard_map/all_gather | solution.py:47
  188.4 68.0 %reduce-scatter.9.cloned.1.call-start = ((), (), s32[]{:S(2)}) async-start(), calls=%async_computation.8 | async-start | bytes 1572864 | tf_op jit(solution)/shard_map/reduce_scatter | solution.py:49
  237.1 121.8 %reduce-scatter.11.cloned.1.call-start = ((), (), s32[]{:S(2)}) async-start(), calls=%async_computation.9 | async-start | bytes 4456448 | tf_op jit(solution)/shard_map/reduce_scatter | solution.py:77
  258.0 23.3 %slice-start = ((s8[8388608]{0:T(1024)(128)(4,1)}), s8[4194304]{0:T(1024)(128)(4,1)S(1)}, s32[]{:S(2)}) async-start(s8[8388608]{0:T(1024)(128)(4,1)} %bitcast.53), calls=%async_computation.10 | async-start | bytes 8388608
  266.7 14.6 %slice-start.1 = ((s8[8388608]{0:T(1024)(128)(4,1)}), s8[4194304]{0:T(1024)(128)(4,1)S(1)}, s32[]{:S(2)}) async-start(s8[8388608]{0:T(1024)(128)(4,1)} %bitcast.53), calls=%async_computation.11 | async-start | bytes 8388608
  280.5 0.8 copy-start.2
  305.2 17.6 %copy-start.3 = (bf16[256,1024]{0,1:T(8,128)(2,1)S(1)}, bf16[256,1024]{0,1:T(8,128)(2,1)}, u32[]{:S(2)}) copy-start(bf16[256,1024]{0,1:T(8,128)(2,1)} %copy-done.2) | copy-start | bytes 1572868
Sparse Core Ops, SparseCore 0:
  10.1 44.1 all-gather.2
  65.3 30.6 reduce-scatter.4
  113.8 72.7 reduce-scatter.6
  189.2 40.4 all-gather.4
  237.2 19.1 reduce-scatter.8
  286.1 72.6 reduce-scatter.10
where the time goes:
time: 369 us; the launch traced here: 367 us
  waiting for transfers between devices  175 us (47%)
  matrix products  62 us (17%)
  local copies, waits for them, and re-layouts  60.9 us (17%)
  other arithmetic  29.9 us (8%)
  blocking collectives  25 us (7%)
  between operations  14.2 us (4%)
    reduce_scatter x1, waiting for transfers between devices, per_device(): lax.psum_scatter(jnp.dot(piece, down_eff, preferred_element_type=jnp.floa...  72.9 us
    unnamed x20, local copies, waits for them, and re-layouts  60.3 us
    all_gather x1, waiting for transfers between devices, per_device(): error_all = lax.all_gather(error, 'hid', axis=0, tiled=True)  41.1 us
    reduce_scatter x1, waiting for transfers between devices, per_device(): lax.psum_scatter(jnp.concatenate([gate_part, up_part], axis=1), 'tok', sc...  23.2 us
    reduce_scatter x1, waiting for transfers between devices, per_device(): lax.psum_scatter(lax.dot_general(piece, down_eff, by_cols, preferred_elem...  19.2 us
    reduce_scatter x1, waiting for transfers between devices, per_device(): lax.psum_scatter(first + lax.dot_general(up_grad_all, up_eff, by_cols, pr...  10.4 us
    dot_general x1, matrix products, per_device(): lax.dot_general(hidden_all, error_all, by_rows, preferred_element_type=jn...  10.3 us
    dot_general x1, matrix products, per_device(): lax.dot_general(inputs_all, gate_grad_all, by_rows, preferred_element_typ...  8.86 us
  transfers between devices with their start and end apart: 6, of which 6 were waited for; matrix products, arithmetic and copies ran while one was open for 30% of the time, Pallas kernels for 0%

commit v1 on v0

v1 whole, which is shorter than its diff:
```python
import functools
import math

import jax
import jax.numpy as jnp
from jax import lax
from jax.experimental import pallas as pl
from jax.experimental.pallas import tpu as pltpu
from jax.sharding import PartitionSpec as P


BLOCK = 128
CORES = 2
F32, BF16 = jnp.float32, jnp.bfloat16
BY_COLS = (((1,), (1,)), ((), ()))
BY_ROWS = (((0,), (0,)), ((), ()))
MIB = 2**20
VM = pl.BlockSpec(memory_space=pltpu.VMEM)
HB = pl.BlockSpec(memory_space=pl.ANY)


def swap(x, axis, offset):
    n = lax.axis_size(axis)
    return lax.ppermute(x, axis, [(i, i ^ offset) for i in range(n)])


def shifts(x):
    n = lax.axis_size("tok")
    return [lax.ppermute(x, "tok", [(i, (i + d) % n) for i in range(n)]) for d in range(1, n)]


def sds(shape, dtype):
    return jax.ShapeDtypeStruct(shape, dtype)


def call(body, outs, args, flops, in_specs=None, out_specs=None, grid=(), scratch=(), limit=8, effects=False, aliases=None):
    moved = sum(a.size * a.dtype.itemsize for a in args)
    moved += sum(math.prod(o.shape) * jnp.dtype(o.dtype).itemsize for o in outs)
    return pl.pallas_call(
        body,
        grid=grid,
        in_specs=in_specs or [VM] * len(args),
        out_specs=out_specs or [VM] * len(outs),
        out_shape=outs,
        scratch_shapes=list(scratch),
        input_output_aliases=aliases or {},
        cost_estimate=pl.CostEstimate(flops=flops, bytes_accessed=moved, transcendentals=0),
        compiler_params=pltpu.CompilerParams(
            vmem_limit_bytes=limit * MIB,
            has_side_effects=effects,
            dimension_semantics=("arbitrary",) * len(grid) if grid else None,
        ),
    )(*args)


def vm(a):
    return pltpu.with_memory_space_constraint(a, pltpu.VMEM)


def whole(a):
    return pl.BlockSpec(a.shape, lambda i: (0,) * a.ndim)


def load_body(w, m, out, sems):
    n = sems.shape[0]
    rows = w.shape[0] // n
    copies = [
        pltpu.make_async_copy(w.at[pl.ds(j * rows, rows), :], out.at[pl.ds(j * rows, rows), :], sems.at[j])
        for j in range(n)
    ]
    for c in copies:
        c.start()
    for j in range(n):
        copies[j].wait()

        @pl.loop(0, rows // BLOCK)
        def _(i):
            k = j * (rows // BLOCK) + i
            at = pl.ds(pl.multiple_of(k * BLOCK, BLOCK), BLOCK)
            out[at, :] = out[at, :] * jnp.broadcast_to(m[k].astype(BF16), (BLOCK, w.shape[1]))


def load(w, m):
    parts = 4 if w.shape[0] % (4 * BLOCK) == 0 else 1
    return call(
        load_body, [pltpu.VMEM(w.shape, BF16)], (pltpu.with_memory_space_constraint(w, pltpu.HBM), m), 0,
        in_specs=[HB, VM], scratch=[pltpu.SemaphoreType.DMA((parts,))], limit=4,
    )[0]


def tick_body(x, out):
    out[...] = jnp.zeros_like(out)


def tick(x):
    return call(tick_body, [pltpu.VMEM((8, BLOCK), F32)], (x,), 0, in_specs=[HB], limit=1, effects=True)


def gate_up_body(x0, x1, ge, ue, own, send):
    x = jnp.concatenate([x0[...], x1[...]], axis=0)
    f = ge.shape[1]
    for w, off in ((ge, 0), (ue, f)):
        part = jnp.dot(x, w[...], preferred_element_type=F32)
        own[:, off : off + f] = part
        send[:, off : off + f] = part.astype(BF16)


def gate_up(x0, x1, ge, ue):
    d, f = ge.shape
    m = 2 * x0.shape[0]
    outs = [sds((m, 2 * f), F32), sds((m, 2 * f), BF16)]
    return call(gate_up_body, outs, (x0, x1, vm(ge), vm(ue)), 4 * m * d * f)


def total(own, recvs):
    out = own[...]
    for r in recvs:
        out = out + r[...].astype(F32)
    return out


def columns(d, n):
    return [slice(c, min(c + n, d)) for c in range(0, d, n)]


def down_body(n, *refs):
    act, recvs = refs[0], refs[1 : 1 + n]
    de, hidden, own, send = refs[1 + n :]
    f, d = de.shape
    both = total(act, recvs)
    gate, up = both[:, :f], both[:, f:]
    h = (gate * jax.nn.sigmoid(gate) * up).astype(BF16)
    hidden[...] = h
    half = own.shape[0]
    for c in columns(d, 1024):
        part = jnp.dot(h, de[:, c], preferred_element_type=F32)
        own[:, c] = part[:half]
        send[:, c] = part[half:].astype(BF16)


def down(act, recvs, de):
    f, d = de.shape
    m = act.shape[0]
    outs = [sds((m, f), BF16), sds((m // 2, d), F32), sds((m // 2, d), BF16)]
    return call(functools.partial(down_body, len(recvs)), outs, (act, *recvs, vm(de)), 2 * m * d * f)


def hidden_grad_body(e0, e1, de, own, send):
    e = jnp.concatenate([e0[...], e1[...]], axis=0)
    for c in columns(de.shape[0], 512):
        part = lax.dot_general(de[c, :], e, BY_COLS, preferred_element_type=F32).T
        own[:, c] = part
        send[:, c] = part.astype(BF16)


def hidden_grad(e0, e1, de):
    f, d = de.shape
    m = 2 * e0.shape[0]
    outs = [sds((m, f), F32), sds((m, f), BF16)]
    return call(hidden_grad_body, outs, (e0, e1, vm(de)), 2 * m * d * f)


def stack(dst, pieces):
    row = 0
    for p in pieces:
        dst[row : row + p.shape[0], :] = p[...]
        row += p.shape[0]


def wgrad_block(ls, right, c, mask, factor, store):
    left = jnp.concatenate([l[:, c] for l in ls], axis=0)
    w = lax.dot_general(left, right[...], BY_ROWS, preferred_element_type=F32)
    for k in range((c.stop - c.start) // BLOCK):
        rows = slice(k * BLOCK, (k + 1) * BLOCK)
        store(rows, w[rows, :] * (mask[c.start // BLOCK + k] * factor))


def input_grad_body(groups, n, *refs):
    acts, refs = [refs[g * (1 + n) : (g + 1) * (1 + n)] for g in range(groups)], refs[groups * (1 + n) :]
    hids, refs = [refs[g * (1 + n) : (g + 1) * (1 + n)] for g in range(groups)], refs[groups * (1 + n) :]
    ge, ue, gg_ref, ug_ref = refs[:4]
    owns, sends = refs[4 : 4 + groups], refs[4 + groups :]
    d, f = ge.shape
    m = gg_ref.shape[0] // groups
    for g, (act, hid) in enumerate(zip(acts, hids)):
        both, hg = total(act[0], act[1:]), total(hid[0], hid[1:])
        gate, up = both[:, :f], both[:, f:]
        sigma = jax.nn.sigmoid(gate)
        swish = gate * sigma
        gg_ref[g * m : (g + 1) * m, :] = (hg * up * (sigma + swish * (1.0 - sigma))).astype(BF16)
        ug_ref[g * m : (g + 1) * m, :] = (hg * swish).astype(BF16)
    for c in columns(d, 1024):
        part = lax.dot_general(ge[c, :], gg_ref[...], BY_COLS, preferred_element_type=F32)
        part += lax.dot_general(ue[c, :], ug_ref[...], BY_COLS, preferred_element_type=F32)
        part = part.T
        for g in range(groups):
            owns[g][:, c] = part[g * m : g * m + m // 2]
            sends[g][:, c] = part[g * m + m // 2 : (g + 1) * m].astype(BF16)


def input_grad(acts, hids, ge, ue):
    d, f = ge.shape
    groups, m, n = len(acts), acts[0][0].shape[0], len(acts[0][1])
    outs = [sds((groups * m, f), BF16)] * 2 + [sds((m // 2, d), F32)] * groups + [sds((m // 2, d), BF16)] * groups
    args = [a for own, recvs in (*acts, *hids) for a in (own, *recvs)] + [vm(ge), vm(ue)]
    gg, ug, *rest = call(functools.partial(input_grad_body, groups, n), outs, args, 4 * groups * m * d * f, limit=12)
    return gg, ug, list(zip(rest[:groups], rest[groups:]))


def wgrad_body(nl, nr, factor, aliased, *refs):
    ls, rs, mask = refs[:nl], refs[nl : nl + nr], refs[nl + nr]
    out, right = refs[nl + nr + 1 + aliased :]

    @pl.when(pl.program_id(0) == 0)
    def _():
        stack(right, rs)

    def store(rows, value):
        out[rows, :] = value

    wgrad_block(ls, right, slice(0, out.shape[0]), mask, factor, store)


def wgrad(ls, rs, mask, factor, size, first, count, prev):
    a, b = ls[0].shape[1], rs[0].shape[1]
    m = sum(l.shape[0] for l in ls)
    specs = [pl.BlockSpec((l.shape[0], size), lambda i: (0, first + i)) for l in ls] + [whole(r) for r in rs]
    specs.append(pl.BlockSpec((size // BLOCK, 1, b), lambda i: (first + i, 0, 0)))
    args = (*ls, *rs, mask)
    if prev is not None:
        args, specs = (*args, prev), specs + [HB]
    return call(
        functools.partial(wgrad_body, len(ls), len(rs), factor, int(prev is not None)), [sds((a, b), F32)],
        args, 2 * m * size * count * b, in_specs=specs,
        out_specs=[pl.BlockSpec((size, b), lambda i: (first + i, 0))],
        grid=(count,), scratch=[pltpu.VMEM((m, b), BF16)], limit=16,
        aliases={} if prev is None else {len(args) - 1: 0},
    )[0]


def gather(shard, zs, xs, ticks):
    column = [shard] + [swap(shard, "hid", z) for z in zs[:2]]
    if zs:
        column.append(swap(column[2], "hid", zs[0]))
    groups = [column] + [[swap(p, "hid", x) for p in column] for x in xs]
    if ticks:
        tick(shard)
        tick(column[2])
    halves = [jnp.concatenate(g, axis=0) for g in groups]
    return [(h, swap(h, "hid", 1)) for h in halves]


def scatter(parts, zs, xs, ticks):
    nz = len(zs) + 1
    sums = [own + swap(send, "hid", 1).astype(F32) for own, send in parts]
    rows = sums[0].shape[0] // nz

    def part(i, k):
        return sums[i][k * rows : (k + 1) * rows]

    def sent(x, offset):
        return swap(x.astype(BF16), "hid", offset).astype(F32)

    out = part(0, 0)
    if not zs:
        for j, x in enumerate(xs):
            out = out + sent(part(j + 1, 0), x)
        return out
    one, two = part(0, 1), part(0, 2) + sent(part(0, 3), zs[0])
    for j, x in enumerate(xs):
        two = two + sent(part(j + 1, 2), x)
    two = two.astype(BF16)
    if ticks:
        tick(two)
    for j, x in enumerate(xs):
        one = one + lax.optimization_barrier((sent(part(j + 1, 1), x), two))[0]
        out = out + sent(part(j + 1, 3), x ^ zs[2]) + sent(part(j + 1, 0), x)
    return out + sent(two, zs[1]) + sent(one, zs[0])


def layer(student_in, target_delta, gw, uw, dw, block_mask):
    hid = lax.axis_size("hid")
    nz = 4 if hid % 8 == 0 else 1
    nx = hid // (nz * CORES)
    zs = [k * nx * CORES for k in range(1, nz)]
    xs = [j * CORES for j in range(1, nx)]
    factor = float((student_in.shape[0] * hid) ** -0.5)

    def wide(b):
        return jnp.repeat(b.astype(F32), BLOCK, axis=1)[:, None, :]

    gm, um, dm = wide(block_mask[0]), wide(block_mask[1]), wide(block_mask[2].T)
    ge, ue, de = load(gw, gm), load(uw, um), load(dw, dm)

    inputs = gather(student_in, zs, xs, False)
    acts = []
    for x0, x1 in inputs:
        own, send = gate_up(x0, x1, ge, ue)
        acts.append((own, shifts(send)))
    hiddens, parts = [], []
    for own, recvs in acts:
        h, o, s = down(own, recvs, de)
        hiddens.append(h)
        parts.append((o, s))
    output_sum = scatter(parts, zs, xs, True)
    error = (output_sum - target_delta.astype(F32)).astype(BF16)
    errors = gather(error, zs, xs, True)
    hgs = []
    for e0, e1 in errors:
        own, send = hidden_grad(e0, e1, de)
        hgs.append((own, shifts(send)))
    all_in = [p for x in inputs for p in x]
    all_err = [p for e in errors for p in e]
    d, f = gw.shape
    dsize, gsize = BLOCK, min(512, d)
    down_w = wgrad(hiddens, all_err, dm, factor, dsize, 0, f // dsize, None)
    gg, ug, parts = input_grad(acts, hgs, ge, ue)
    gate_w = wgrad(all_in, [gg], gm, factor, gsize, 0, d // gsize, None)
    up_w = wgrad(all_in, [ug], um, factor, gsize, 0, d // gsize, None)
    grad = scatter(parts, zs, xs, False)
    return (output_sum.astype(BF16), grad.astype(BF16), gate_w, up_w, down_w)


def solution(mesh):
    placed = (
        P("hid", "tok"),
        P("hid", "tok"),
        P("tok", "hid"),
        P("tok", "hid"),
        P("hid", "tok"),
        P(None, "tok", "hid"),
    )
    return jax.shard_map(
        layer,
        mesh=mesh,
        in_specs=placed,
        out_specs=(
            P("hid", "tok"),
            P("hid", "tok"),
            P("tok", "hid"),
            P("tok", "hid"),
            P("hid", "tok"),
        ),
        check_vma=False,
    )
```

time: 369 us -> 163 us (0.44)
  waiting for transfers between devices: 175 us -> 69.2 us
  matrix products: 62 us -> 0 us
  local copies, waits for them, and re-layouts: 60.9 us -> 1.58 us
  Pallas kernels: 0 us -> 54.3 us
  starting transfers between devices: 0.42 us -> 34.3 us
  other arithmetic: 29.9 us -> 2.79 us
  blocking collectives: 25 us -> 0 us
  between operations: 14.2 us -> 1.06 us
    reduce_scatter x4 -> x0, waiting for transfers between devices: 126 us -> none  [the longest x1 72.9 us: per_device(): lax.psum_scatter(jnp.dot(piece, down_eff, preferred_element_type=jnp.floa...]
    ppermute x0 -> x40, waiting for transfers between devices: none -> 69.2 us  [the longest x36 43.7 us: swap(): return lax.ppermute(x, axis, [(i, i ^ offset) for i in range(n)])]
    dot_general x9 -> x0, matrix products: 62 us -> none  [the longest x1 10.3 us: per_device(): lax.dot_general(hidden_all, error_all, by_rows, preferred_element_type=jn...]
    unnamed x20 -> x11, local copies, waits for them, and re-layouts: 60.3 us -> 1.03 us
    pallas_call x0 -> x16, Pallas kernels: none -> 54.3 us  [call(): pl.pallas_call(body, grid=grid, in_specs=in_specs or [VM] * len(args), ou...]
    all_gather x2 -> x0, waiting for transfers between devices: 48.5 us -> none  [the longest x1 41.1 us: per_device(): error_all = lax.all_gather(error, 'hid', axis=0, tiled=True)]
    ppermute x0 -> x40, starting transfers between devices: none -> 34.3 us  [the longest x36 29.9 us: swap(): return lax.ppermute(x, axis, [(i, i ^ offset) for i in range(n)])]
    all_gather x3 -> x0, blocking collectives: 25 us -> none  [the longest x1 8.7 us: per_device(): lax.all_gather(gate_grad, 'tok', axis=0, tiled=True)]
  transfers between devices with their start and end apart: 6 -> 40, of which waited for: 6 -> 19; matrix products, arithmetic and copies ran while one was open for 30% -> 2% of each run, Pallas kernels for 0% -> 30%
where the time goes in v1:
time: 163 us
  waiting for transfers between devices  69.2 us (42%)
  Pallas kernels  54.3 us (33%)
  starting transfers between devices  34.3 us (21%)
  other arithmetic  2.79 us (2%)
    pallas_call x16, Pallas kernels, call(): pl.pallas_call(body, grid=grid, in_specs=in_specs or [VM] * len(args), ou...  54.3 us
    ppermute x36, waiting for transfers between devices, swap(): return lax.ppermute(x, axis, [(i, i ^ offset) for i in range(n)])  43.7 us
    ppermute x36, starting transfers between devices, swap(): return lax.ppermute(x, axis, [(i, i ^ offset) for i in range(n)])  29.9 us
    ppermute x4, waiting for transfers between devices, shifts(): lax.ppermute(x, 'tok', [(i, (i + d) % n) for i in range(n)])  25.5 us
    ppermute x4, starting transfers between devices, shifts(): lax.ppermute(x, 'tok', [(i, (i + d) % n) for i in range(n)])  4.33 us
  transfers between devices with their start and end apart: 40, of which 19 were waited for; matrix products, arithmetic and copies ran while one was open for 2% of the time, Pallas kernels for 30%

profile of v1, /device:TPU:0, one launch (start us, length us, event | category | flops | bytes accessed | tf_op | source)
XLA Modules:
  0.0 163.2 jit_solution(10811089995335309144)
XLA Ops:
  0.6 4.1 %collective-permute-start.1 = (bf16[16,4096]{1,0:T(8,128)(2,1)}, bf16[16,4096]{1,0:T(8,128)(2,1)S(1)}, u32[]{:S(2)}, u32[]{:S(2)}) collective-permute-start(bf16[16,4096]{1,0:T(8,128)(2,1)} %param.6), channel_id=1, source_target_pairs={{0,8},{1,9},{2,10},{3,11},{4,12},{5,13},{6,14},{7,15},{8,0},{9,1},... | collective-permute-start | bytes 393224 | tf_op jit(solution)/shard_map/ppermute | solution.py:24
  4.8 1.6 collective-permute-start
  6.3 1.5 collective-permute-start.7
  7.8 0.9 constant_dynamic-update-slice_fusion.3
  8.8 0.7 convert_bitcast_fusion
  9.8 3.7 %shard_map.101.ge.refs_8_ = bf16[4096,1024]{1,0:T(8,128)(2,1)S(1)} custom-call(bf16[4096,1024]{1,0:T(8,128)(2,1)} %w.3, f32[32,1,1024]{2,1,0:T(1,128)S(1)} %bitcast.13), custom_call_target="tpu_custom_call" | custom-call | bytes 16908288 | tf_op jit(solution)/shard_map/pallas_call | solution.py:39
  13.5 3.7 %shard_map.102.ue.refs_9_ = bf16[4096,1024]{1,0:T(8,128)(2,1)S(1)} custom-call(bf16[4096,1024]{1,0:T(8,128)(2,1)} %w.4, f32[32,1,1024]{2,1,0:T(1,128)S(1)} %bitcast.11), custom_call_target="tpu_custom_call" | custom-call | bytes 16908288 | tf_op jit(solution)/shard_map/pallas_call | solution.py:39
  17.3 0.6 collective-permute-start.9
  17.9 0.4 collective-permute-start.2
  18.3 1.5 collective-permute-start.8
  19.9 3.0 %collective-permute-done.2 = bf16[16,4096]{1,0:T(8,128)(2,1)S(1)} collective-permute-done((bf16[16,4096]{1,0:T(8,128)(2,1)S(1)}, bf16[16,4096]{1,0:T(8,128)(2,1)S(1)}, u32[]{:S(2)}, u32[]{:S(2)}) %collective-permute-start.2) | collective-permute-done | bytes 131104 | tf_op jit(solution)/shard_map/ppermute | solution.py:24
  22.9 1.6 collective-permute-start.10
  24.6 4.2 %collective-permute-done.10 = bf16[16,4096]{1,0:T(8,128)(2,1)S(1)} collective-permute-done((bf16[16,4096]{1,0:T(8,128)(2,1)S(1)}, bf16[16,4096]{1,0:T(8,128)(2,1)S(1)}, u32[]{:S(2)}, u32[]{:S(2)}) %collective-permute-start.10) | collective-permute-done | bytes 131104 | tf_op jit(solution)/shard_map/ppermute | solution.py:24
  28.9 2.3 %shard_map.103 = (f32[128,2048]{1,0:T(8,128)S(1)}, bf16[128,2048]{1,0:T(8,128)(2,1)S(1)}) custom-call(bf16[64,4096]{1,0:T(8,128)(2,1)S(1)} %constant_dynamic-update-slice_fusion.x0.refs_0_, bf16[64,4096]{1,0:T(8,128)(2,1)S(1)} %collective-permute-done.3.x1.refs_1_, bf16[4096,1024]{1,0:T(8,128)(2,1)S(1)} %shard_map.101.ge.refs_8_, ...), custom_call_target="tpu_custom_call" | custom-call | flops 2147483648 | bytes 19398656 | tf_op jit(solution)/shard_map/pallas_call | solution.py:39
  31.3 1.6 collective-permute-start.4
  32.9 3.8 %shard_map.104.refs_2_.de = bf16[1024,4096]{1,0:T(8,128)(2,1)S(1)} custom-call(bf16[1024,4096]{1,0:T(8,128)(2,1)} %w.5, f32[8,1,4096]{2,1,0:T(1,128)S(1)} %bitcast.15), custom_call_target="tpu_custom_call" | custom-call | bytes 16908288 | tf_op jit(solution)/shard_map/pallas_call | solution.py:39
  36.8 2.3 %shard_map.106 = (f32[128,2048]{1,0:T(8,128)S(1)}, bf16[128,2048]{1,0:T(8,128)(2,1)S(1)}) custom-call(bf16[64,4096]{1,0:T(8,128)(2,1)S(1)} %constant_dynamic-update-slice_fusion.4.x0.refs_2_, bf16[64,4096]{1,0:T(8,128)(2,1)S(1)} %collective-permute-done.11.x1.refs_3_, bf16[4096,1024]{1,0:T(8,128)(2,1)S(1)} %shard_map.101.ge.refs_8_, ...), custom_call_target="tpu_custom_call" | custom-call | flops 2147483648 | bytes 19398656 | tf_op jit(solution)/shard_map/pallas_call | solution.py:39
  39.2 0.6 collective-permute-start.12
  39.7 6.4 %collective-permute-done.4.refs_1_ = bf16[128,2048]{1,0:T(8,128)(2,1)S(1)} collective-permute-done((bf16[128,2048]{1,0:T(8,128)(2,1)S(1)}, bf16[128,2048]{1,0:T(8,128)(2,1)S(1)}, u32[]{:S(2)}, u32[]{:S(2)}) %collective-permute-start.4) | collective-permute-done | bytes 524320 | tf_op jit(solution)/shard_map/ppermute | solution.py:29
  46.1 1.3 shard_map.105
  47.5 9.4 %collective-permute-done.12.refs_1_.refs_3_ = bf16[128,2048]{1,0:T(8,128)(2,1)S(1)} collective-permute-done((bf16[128,2048]{1,0:T(8,128)(2,1)S(1)}, bf16[128,2048]{1,0:T(8,128)(2,1)S(1)}, u32[]{:S(2)}, u32[]{:S(2)}) %collective-permute-start.12) | collective-permute-done | bytes 524320 | tf_op jit(solution)/shard_map/ppermute | solution.py:29
  56.9 1.3 shard_map.107
  58.4 1.8 %collective-permute-done.13 = bf16[64,4096]{1,0:T(8,128)(2,1)S(1)} collective-permute-done((bf16[64,4096]{1,0:T(8,128)(2,1)S(1)}, bf16[64,4096]{1,0:T(8,128)(2,1)S(1)}, u32[]{:S(2)}, u32[]{:S(2)}) %collective-permute-start.13) | collective-permute-done | bytes 524320 | tf_op jit(solution)/shard_map/ppermute | solution.py:24
  60.3 1.6 collective-permute-start.18
  61.9 0.4 collective-permute-start.6
  62.3 0.5 collective-permute-start.14
  62.9 2.3 %collective-permute-start.15 = (bf16[16,4096]{1,0:T(8,128)(2,1)S(1)}, bf16[16,4096]{1,0:T(8,128)(2,1)S(1)}, u32[]{:S(2)}, u32[]{:S(2)}) collective-permute-start(bf16[16,4096]{1,0:T(8,128)(2,1)S(1)} %get-tuple-element.55), channel_id=1, source_target_pairs={{0,14},{1,15},{2,12},{3,13},{4,10},{5,11},{6,8},{7,9},{8,6},{9,7},... | collective-permute-start | bytes 393224 | tf_op jit(solution)/shard_map/ppermute | solution.py:24
  65.1 0.5 collective-permute-start.16
  65.7 1.1 collective-permute-done.18
  67.1 5.2 %collective-permute-done.14 = bf16[16,4096]{1,0:T(8,128)(2,1)S(1)} collective-permute-done((bf16[16,4096]{1,0:T(8,128)(2,1)S(1)}, bf16[16,4096]{1,0:T(8,128)(2,1)S(1)}, u32[]{:S(2)}, u32[]{:S(2)}) %collective-permute-start.14) | collective-permute-done | bytes 131104 | tf_op jit(solution)/shard_map/ppermute | solution.py:24
  72.9 1.4 collective-permute-done.16
  74.4 4.2 %collective-permute-done.19 = bf16[16,4096]{1,0:T(8,128)(2,1)S(1)} collective-permute-done((bf16[16,4096]{1,0:T(8,128)(2,1)S(1)}, bf16[16,4096]{1,0:T(8,128)(2,1)S(1)}, u32[]{:S(2)}, u32[]{:S(2)}) %collective-permute-start.19) | collective-permute-done | bytes 131104 | tf_op jit(solution)/shard_map/ppermute | solution.py:24
  78.6 1.9 %collective-permute-done.17 = bf16[16,4096]{1,0:T(8,128)(2,1)S(1)} collective-permute-done((bf16[16,4096]{1,0:T(8,128)(2,1)S(1)}, bf16[16,4096]{1,0:T(8,128)(2,1)S(1)}, u32[]{:S(2)}, u32[]{:S(2)}) %collective-permute-start.17) | collective-permute-done | bytes 131104 | tf_op jit(solution)/shard_map/ppermute | solution.py:24
  80.5 0.8 subtract_convert_fusion
  81.2 1.8 %collective-permute-start.21 = (bf16[16,4096]{1,0:T(8,128)(2,1)S(1)}, bf16[16,4096]{1,0:T(8,128)(2,1)S(1)}, u32[]{:S(2)}, u32[]{:S(2)}) collective-permute-start(bf16[16,4096]{1,0:T(8,128)(2,1)S(1)} %get-tuple-element.49.x), channel_id=1, source_target_pairs={{0,4},{1,5},{2,6},{3,7},{4,0},{5,1},{6,2},{7,3},{8,12},{9,13},{10,... | collective-permute-start | bytes 393224 | tf_op jit(solution)/shard_map/ppermute | solution.py:24
  83.0 1.5 collective-permute-start.25
  84.5 3.5 %collective-permute-done.20.x = bf16[16,4096]{1,0:T(8,128)(2,1)S(1)} collective-permute-done((bf16[16,4096]{1,0:T(8,128)(2,1)S(1)}, bf16[16,4096]{1,0:T(8,128)(2,1)S(1)}, u32[]{:S(2)}, u32[]{:S(2)}) %collective-permute-start.20) | collective-permute-done | bytes 131104 | tf_op jit(solution)/shard_map/ppermute | solution.py:24
  88.0 1.5 collective-permute-start.27
  89.5 0.5 collective-permute-start.26
  90.1 4.4 %collective-permute-done.22 = bf16[16,4096]{1,0:T(8,128)(2,1)S(1)} collective-permute-done((bf16[16,4096]{1,0:T(8,128)(2,1)S(1)}, bf16[16,4096]{1,0:T(8,128)(2,1)S(1)}, u32[]{:S(2)}, u32[]{:S(2)}) %collective-permute-start.22) | collective-permute-done | bytes 131104 | tf_op jit(solution)/shard_map/ppermute | solution.py:24
  94.6 0.6 collective-permute-start.28
  95.3 5.2 %collective-permute-done.28 = bf16[16,4096]{1,0:T(8,128)(2,1)S(1)} collective-permute-done((bf16[16,4096]{1,0:T(8,128)(2,1)S(1)}, bf16[16,4096]{1,0:T(8,128)(2,1)S(1)}, u32[]{:S(2)}, u32[]{:S(2)}) %collective-permute-start.28) | collective-permute-done | bytes 131104 | tf_op jit(solution)/shard_map/ppermute | solution.py:24
  100.6 2.4 %shard_map.111 = (f32[128,1024]{1,0:T(8,128)S(1)}, bf16[128,1024]{1,0:T(8,128)(2,1)S(1)}) custom-call(bf16[64,4096]{1,0:T(8,128)(2,1)S(1)} %pad_maximum_fusion.e0.refs_2_, bf16[64,4096]{1,0:T(8,128)(2,1)S(1)} %collective-permute-done.23.e1.refs_3_, bf16[1024,4096]{1,0:T(8,128)(2,1)S(1)} %shard_map.104.refs_2_.de), custom_call_target="tpu_custom_call" | custom-call | flops 1073741824 | bytes 10223616 | tf_op jit(solution)/shard_map/pallas_call | solution.py:39
  103.0 1.6 collective-permute-start.24
  104.6 2.4 %shard_map.112 = (f32[128,1024]{1,0:T(8,128)S(1)}, bf16[128,1024]{1,0:T(8,128)(2,1)S(1)}) custom-call(bf16[64,4096]{1,0:T(8,128)(2,1)S(1)} %constant_dynamic-update-slice_fusion.8.e0.refs_4_, bf16[64,4096]{1,0:T(8,128)(2,1)S(1)} %collective-permute-done.29.e1.refs_5_, bf16[1024,4096]{1,0:T(8,128)(2,1)S(1)} %shard_map.104.refs_2_.de), custom_call_target="tpu_custom_call" | custom-call | flops 1073741824 | bytes 10223616 | tf_op jit(solution)/shard_map/pallas_call | solution.py:39
  107.1 0.6 collective-permute-start.30
  107.6 4.6 %collective-permute-done.24.refs_5_ = bf16[128,1024]{1,0:T(8,128)(2,1)S(1)} collective-permute-done((bf16[128,1024]{1,0:T(8,128)(2,1)S(1)}, bf16[128,1024]{1,0:T(8,128)(2,1)S(1)}, u32[]{:S(2)}, u32[]{:S(2)}) %collective-permute-start.24) | collective-permute-done | bytes 262176 | tf_op jit(solution)/shard_map/ppermute | solution.py:29
  112.3 5.1 %collective-permute-done.30.refs_7_ = bf16[128,1024]{1,0:T(8,128)(2,1)S(1)} collective-permute-done((bf16[128,1024]{1,0:T(8,128)(2,1)S(1)}, bf16[128,1024]{1,0:T(8,128)(2,1)S(1)}, u32[]{:S(2)}, u32[]{:S(2)}) %collective-permute-start.30) | collective-permute-done | bytes 262176 | tf_op jit(solution)/shard_map/ppermute | solution.py:29
  117.4 5.1 %shard_map.113 = (bf16[256,1024]{1,0:T(8,128)(2,1)S(1)}, bf16[256,1024]{1,0:T(8,128)(2,1)S(1)}, f32[64,4096]{1,0:T(8,128)S(1)}, f32[64,4096]{1,0:T(8,128)S(1)}, ...) custom-call(f32[128,2048]{1,0:T(8,128)S(1)} %get-tuple-element.27.refs_0_, ...), custom_call_target="tpu_custom_call" | custom-call | flops 4294967296 | bytes 25690112 | tf_op jit(solution)/shard_map/pallas_call | solution.py:39
  122.7 0.6 shard_map.108
  123.3 0.6 shard_map.109
  123.8 0.6 shard_map.110
  124.4 8.1 %shard_map.116 = f32[1024,4096]{1,0:T(8,128)} custom-call(bf16[128,1024]{1,0:T(8,128)(2,1)S(1)} %get-tuple-element.47.refs_0_, bf16[128,1024]{1,0:T(8,128)(2,1)S(1)} %get-tuple-element.48.refs_1_, bf16[64,4096]{1,0:T(8,128)(2,1)S(1)} %pad_maximum_fusion.e0.refs_2_, bf16[64,4096]{1,0:T(8,128)(2,1)S(1)} %collective-permute-done.23.e1.refs_3_, ...), custom_call_target="tpu_custom_call" | custom-call | flops 2147483648 | bytes 19529728 | tf_op jit(solution)/shard_map/pallas_call | solution.py:39
  132.5 0.5 collective-permute-start.32
  133.2 1.3 collective-permute-done.32
  134.7 0.6 collective-permute-start.36
  135.3 8.0 %shard_map.114 = f32[4096,1024]{1,0:T(8,128)} custom-call(bf16[64,4096]{1,0:T(8,128)(2,1)S(1)} %constant_dynamic-update-slice_fusion.x0.refs_0_, bf16[64,4096]{1,0:T(8,128)(2,1)S(1)} %collective-permute-done.3.x1.refs_1_, bf16[64,4096]{1,0:T(8,128)(2,1)S(1)} %constant_dynamic-update-slice_fusion.4.x0.refs_2_, ...), custom_call_target="tpu_custom_call" | custom-call | flops 2147483648 | bytes 19529728 | tf_op jit(solution)/shard_map/pallas_call | solution.py:39
  143.2 2.4 %collective-permute-start.33 = (bf16[16,4096]{1,0:T(8,128)(2,1)S(1)}, bf16[16,4096]{1,0:T(8,128)(2,1)S(1)}, u32[]{:S(2)}, u32[]{:S(2)}) collective-permute-start(bf16[16,4096]{1,0:T(8,128)(2,1)S(1)} %get-tuple-element.51), channel_id=1, source_target_pairs={{0,14},{1,15},{2,12},{3,13},{4,10},{5,11},{6,8},{7,9},{8,6},{9,7},... | collective-permute-start | bytes 393224 | tf_op jit(solution)/shard_map/ppermute | solution.py:24
  145.6 0.6 collective-permute-start.38
  146.2 1.5 collective-permute-start.34
  147.7 0.8 collective-permute-start.37
  148.5 5.9 %collective-permute-done.38 = bf16[16,4096]{1,0:T(8,128)(2,1)S(1)} collective-permute-done((bf16[16,4096]{1,0:T(8,128)(2,1)S(1)}, bf16[16,4096]{1,0:T(8,128)(2,1)S(1)}, u32[]{:S(2)}, u32[]{:S(2)}) %collective-permute-start.38) | collective-permute-done | bytes 131104 | tf_op jit(solution)/shard_map/ppermute | solution.py:24
  154.5 8.0 %shard_map.115 = f32[4096,1024]{1,0:T(8,128)} custom-call(bf16[64,4096]{1,0:T(8,128)(2,1)S(1)} %constant_dynamic-update-slice_fusion.x0.refs_0_, bf16[64,4096]{1,0:T(8,128)(2,1)S(1)} %collective-permute-done.3.x1.refs_1_, bf16[64,4096]{1,0:T(8,128)(2,1)S(1)} %constant_dynamic-update-slice_fusion.4.x0.refs_2_, ...), custom_call_target="tpu_custom_call" | custom-call | flops 2147483648 | bytes 19529728 | tf_op jit(solution)/shard_map/pallas_call | solution.py:39
  162.5 0.7 fusion.6
  (69 shorter events, 2.8 us)
Async XLA Ops:
  0.6 16.6 %collective-permute-start.1 = (bf16[16,4096]{1,0:T(8,128)(2,1)}, bf16[16,4096]{1,0:T(8,128)(2,1)S(1)}, u32[]{:S(2)}, u32[]{:S(2)}) collective-permute-start(bf16[16,4096]{1,0:T(8,128)(2,1)} %param.6), channel_id=1, source_target_pairs={{0,8},{1,9},{2,10},{3,11},{4,12},{5,13},{6,14},{7,15},{8,0},{9,1},... | collective-permute-start | bytes 393224 | tf_op jit(solution)/shard_map/ppermute | solution.py:24
  4.8 13.6 %collective-permute-start = (bf16[16,4096]{1,0:T(8,128)(2,1)}, bf16[16,4096]{1,0:T(8,128)(2,1)S(1)}, u32[]{:S(2)}, u32[]{:S(2)}) collective-permute-start(bf16[16,4096]{1,0:T(8,128)(2,1)} %param.6), channel_id=1, source_target_pairs={{0,4},{1,5},{2,6},{3,7},{4,0},{5,1},{6,2},{7,3},{8,12},{9,13},{10,... | collective-permute-start | bytes 393224 | tf_op jit(solution)/shard_map/ppermute | solution.py:24
  6.3 13.5 %collective-permute-start.7 = (bf16[16,4096]{1,0:T(8,128)(2,1)}, bf16[16,4096]{1,0:T(8,128)(2,1)S(1)}, u32[]{:S(2)}, u32[]{:S(2)}) collective-permute-start(bf16[16,4096]{1,0:T(8,128)(2,1)} %param.6), channel_id=1, source_target_pairs={{0,2},{1,3},{2,0},{3,1},{4,6},{5,7},{6,4},{7,5},{8,10},{9,11},{10,... | collective-permute-start | bytes 393224 | tf_op jit(solution)/shard_map/ppermute | solution.py:24
  17.3 7.3 %collective-permute-start.9 = (bf16[16,4096]{1,0:T(8,128)(2,1)S(1)}, bf16[16,4096]{1,0:T(8,128)(2,1)S(1)}, u32[]{:S(2)}, u32[]{:S(2)}) collective-permute-start(bf16[16,4096]{1,0:T(8,128)(2,1)S(1)} %collective-permute-done.1), channel_id=1, source_target_pairs={{0,2},{1,3},{2,0},{3,1},{4,6},{5,7},{6,4},{7,5},{8,10},{9,11},{10,... | collective-permute-start | bytes 393224 | tf_op jit(solution)/shard_map/ppermute | solution.py:24
  17.9 5.0 %collective-permute-start.2 = (bf16[16,4096]{1,0:T(8,128)(2,1)S(1)}, bf16[16,4096]{1,0:T(8,128)(2,1)S(1)}, u32[]{:S(2)}, u32[]{:S(2)}) collective-permute-start(bf16[16,4096]{1,0:T(8,128)(2,1)S(1)} %collective-permute-done.1), channel_id=1, source_target_pairs={{0,4},{1,5},{2,6},{3,7},{4,0},{5,1},{6,2},{7,3},{8,12},{9,13},{10,... | collective-permute-start | bytes 393224 | tf_op jit(solution)/shard_map/ppermute | solution.py:24
  18.3 6.2 %collective-permute-start.8 = (bf16[16,4096]{1,0:T(8,128)(2,1)S(1)}, bf16[16,4096]{1,0:T(8,128)(2,1)S(1)}, u32[]{:S(2)}, u32[]{:S(2)}) collective-permute-start(bf16[16,4096]{1,0:T(8,128)(2,1)S(1)} %collective-permute-done), channel_id=1, source_target_pairs={{0,2},{1,3},{2,0},{3,1},{4,6},{5,7},{6,4},{7,5},{8,10},{9,11},{10,... | collective-permute-start | bytes 393224 | tf_op jit(solution)/shard_map/ppermute | solution.py:24
  22.8 6.1 %collective-permute-start.3 = (bf16[64,4096]{1,0:T(8,128)(2,1)S(1)}, bf16[64,4096]{1,0:T(8,128)(2,1)S(1)}, u32[]{:S(2)}, u32[]{:S(2)}) collective-permute-start(bf16[64,4096]{1,0:T(8,128)(2,1)S(1)} %constant_dynamic-update-slice_fusion.x0.refs_0_), channel_id=1, source_target_pairs={{0,1},{1,0},{2,3},{3,2},{4,5},{5,4},{6,7},{7,6},{8,9},{9,8},{10,11... | collective-permute-start | bytes 1572872 | tf_op jit(solution)/shard_map/ppermute | solution.py:24
  22.9 5.9 %collective-permute-start.10 = (bf16[16,4096]{1,0:T(8,128)(2,1)S(1)}, bf16[16,4096]{1,0:T(8,128)(2,1)S(1)}, u32[]{:S(2)}, u32[]{:S(2)}) collective-permute-start(bf16[16,4096]{1,0:T(8,128)(2,1)S(1)} %collective-permute-done.2), channel_id=1, source_target_pairs={{0,2},{1,3},{2,0},{3,1},{4,6},{5,7},{6,4},{7,5},{8,10},{9,11},{10,... | collective-permute-start | bytes 393224 | tf_op jit(solution)/shard_map/ppermute | solution.py:24
  28.8 8.0 %collective-permute-start.11 = (bf16[64,4096]{1,0:T(8,128)(2,1)S(1)}, bf16[64,4096]{1,0:T(8,128)(2,1)S(1)}, u32[]{:S(2)}, u32[]{:S(2)}) collective-permute-start(bf16[64,4096]{1,0:T(8,128)(2,1)S(1)} %constant_dynamic-update-slice_fusion.4.x0.refs_2_), channel_id=1, source_target_pairs={{0,1},{1,0},{2,3},{3,2},{4,5},{5,4},{6,7},{7,6},{8,9},{9,8},{10,11... | collective-permute-start | bytes 1572872 | tf_op jit(solution)/shard_map/ppermute | solution.py:24
  31.3 14.9 %collective-permute-start.4 = (bf16[128,2048]{1,0:T(8,128)(2,1)S(1)}, bf16[128,2048]{1,0:T(8,128)(2,1)S(1)}, u32[]{:S(2)}, u32[]{:S(2)}) collective-permute-start(bf16[128,2048]{1,0:T(8,128)(2,1)S(1)} %get-tuple-element.28), channel_id=1, source_target_pairs={{0,16},{16,0},{1,17},{17,1},{2,18},{18,2},{3,19},{19,3},{4,20},{20... | collective-permute-start | bytes 1572872 | tf_op jit(solution)/shard_map/ppermute | solution.py:29
  39.2 17.7 %collective-permute-start.12 = (bf16[128,2048]{1,0:T(8,128)(2,1)S(1)}, bf16[128,2048]{1,0:T(8,128)(2,1)S(1)}, u32[]{:S(2)}, u32[]{:S(2)}) collective-permute-start(bf16[128,2048]{1,0:T(8,128)(2,1)S(1)} %get-tuple-element.32), channel_id=1, source_target_pairs={{0,16},{16,0},{1,17},{17,1},{2,18},{18,2},{3,19},{19,3},{4,20},{20... | collective-permute-start | bytes 1572872 | tf_op jit(solution)/shard_map/ppermute | solution.py:29
  47.4 10.8 %collective-permute-start.5 = (bf16[64,4096]{1,0:T(8,128)(2,1)S(1)}, bf16[64,4096]{1,0:T(8,128)(2,1)S(1)}, u32[]{:S(2)}, u32[]{:S(2)}) collective-permute-start(bf16[64,4096]{1,0:T(8,128)(2,1)S(1)} %get-tuple-element.30), channel_id=1, source_target_pairs={{0,1},{1,0},{2,3},{3,2},{4,5},{5,4},{6,7},{7,6},{8,9},{9,8},{10,11... | collective-permute-start | bytes 1572872 | tf_op jit(solution)/shard_map/ppermute | solution.py:24
  56.9 23.6 %copy-start = (bf16[16,4096]{1,0:T(8,128)(2,1)S(1)}, bf16[16,4096]{1,0:T(8,128)(2,1)}, u32[]{:S(2)}) copy-start(bf16[16,4096]{1,0:T(8,128)(2,1)} %param.7) | copy-start | bytes 393220
  58.2 2.0 %collective-permute-start.13 = (bf16[64,4096]{1,0:T(8,128)(2,1)S(1)}, bf16[64,4096]{1,0:T(8,128)(2,1)S(1)}, u32[]{:S(2)}, u32[]{:S(2)}) collective-permute-start(bf16[64,4096]{1,0:T(8,128)(2,1)S(1)} %get-tuple-element.34), channel_id=1, source_target_pairs={{0,1},{1,0},{2,3},{3,2},{4,5},{5,4},{6,7},{7,6},{8,9},{9,8},{10,11... | collective-permute-start | bytes 1572872 | tf_op jit(solution)/shard_map/ppermute | solution.py:24
  60.3 6.4 %collective-permute-start.18 = (bf16[16,4096]{1,0:T(8,128)(2,1)S(1)}, bf16[16,4096]{1,0:T(8,128)(2,1)S(1)}, u32[]{:S(2)}, u32[]{:S(2)}) collective-permute-start(bf16[16,4096]{1,0:T(8,128)(2,1)S(1)} %get-tuple-element.56), channel_id=1, source_target_pairs={{0,2},{1,3},{2,0},{3,1},{4,6},{5,7},{6,4},{7,5},{8,10},{9,11},{10,... | collective-permute-start | bytes 393224 | tf_op jit(solution)/shard_map/ppermute | solution.py:24
  61.9 5.3 %collective-permute-start.6 = (bf16[16,4096]{1,0:T(8,128)(2,1)S(1)}, bf16[16,4096]{1,0:T(8,128)(2,1)S(1)}, u32[]{:S(2)}, u32[]{:S(2)}) collective-permute-start(bf16[16,4096]{1,0:T(8,128)(2,1)S(1)} %slice.144), channel_id=1, source_target_pairs={{0,4},{1,5},{2,6},{3,7},{4,0},{5,1},{6,2},{7,3},{8,12},{9,13},{10,... | collective-permute-start | bytes 393224 | tf_op jit(solution)/shard_map/ppermute | solution.py:24
  62.3 10.0 %collective-permute-start.14 = (bf16[16,4096]{1,0:T(8,128)(2,1)S(1)}, bf16[16,4096]{1,0:T(8,128)(2,1)S(1)}, u32[]{:S(2)}, u32[]{:S(2)}) collective-permute-start(bf16[16,4096]{1,0:T(8,128)(2,1)S(1)} %get-tuple-element.58), channel_id=1, source_target_pairs={{0,2},{1,3},{2,0},{3,1},{4,6},{5,7},{6,4},{7,5},{8,10},{9,11},{10,... | collective-permute-start | bytes 393224 | tf_op jit(solution)/shard_map/ppermute | solution.py:24
  62.9 10.1 %collective-permute-start.15 = (bf16[16,4096]{1,0:T(8,128)(2,1)S(1)}, bf16[16,4096]{1,0:T(8,128)(2,1)S(1)}, u32[]{:S(2)}, u32[]{:S(2)}) collective-permute-start(bf16[16,4096]{1,0:T(8,128)(2,1)S(1)} %get-tuple-element.55), channel_id=1, source_target_pairs={{0,14},{1,15},{2,12},{3,13},{4,10},{5,11},{6,8},{7,9},{8,6},{9,7},... | collective-permute-start | bytes 393224 | tf_op jit(solution)/shard_map/ppermute | solution.py:24
  65.1 9.2 %collective-permute-start.16 = (bf16[16,4096]{1,0:T(8,128)(2,1)S(1)}, bf16[16,4096]{1,0:T(8,128)(2,1)S(1)}, u32[]{:S(2)}, u32[]{:S(2)}) collective-permute-start(bf16[16,4096]{1,0:T(8,128)(2,1)S(1)} %get-tuple-element.57), channel_id=1, source_target_pairs={{0,2},{1,3},{2,0},{3,1},{4,6},{5,7},{6,4},{7,5},{8,10},{9,11},{10,... | collective-permute-start | bytes 393224 | tf_op jit(solution)/shard_map/ppermute | solution.py:24
  72.5 6.1 %collective-permute-start.19 = (bf16[16,4096]{1,0:T(8,128)(2,1)S(1)}, bf16[16,4096]{1,0:T(8,128)(2,1)S(1)}, u32[]{:S(2)}, u32[]{:S(2)}) collective-permute-start(bf16[16,4096]{1,0:T(8,128)(2,1)S(1)} %fusion.7), channel_id=1, source_target_pairs={{0,4},{1,5},{2,6},{3,7},{4,0},{5,1},{6,2},{7,3},{8,12},{9,13},{10,... | collective-permute-start | bytes 393224 | tf_op jit(solution)/shard_map/ppermute | solution.py:24
  72.5 7.9 %collective-permute-start.17 = (bf16[16,4096]{1,0:T(8,128)(2,1)S(1)}, bf16[16,4096]{1,0:T(8,128)(2,1)S(1)}, u32[]{:S(2)}, u32[]{:S(2)}) collective-permute-start(bf16[16,4096]{1,0:T(8,128)(2,1)S(1)} %fusion.9.x), channel_id=1, source_target_pairs={{0,8},{1,9},{2,10},{3,11},{4,12},{5,13},{6,14},{7,15},{8,0},{9,1},... | collective-permute-start | bytes 393224 | tf_op jit(solution)/shard_map/ppermute | solution.py:24
  81.2 6.8 %collective-permute-start.20 = (bf16[16,4096]{1,0:T(8,128)(2,1)S(1)}, bf16[16,4096]{1,0:T(8,128)(2,1)S(1)}, u32[]{:S(2)}, u32[]{:S(2)}) collective-permute-start(bf16[16,4096]{1,0:T(8,128)(2,1)S(1)} %get-tuple-element.49.x), channel_id=1, source_target_pairs={{0,8},{1,9},{2,10},{3,11},{4,12},{5,13},{6,14},{7,15},{8,0},{9,1},... | collective-permute-start | bytes 393224 | tf_op jit(solution)/shard_map/ppermute | solution.py:24
  81.2 8.3 %collective-permute-start.21 = (bf16[16,4096]{1,0:T(8,128)(2,1)S(1)}, bf16[16,4096]{1,0:T(8,128)(2,1)S(1)}, u32[]{:S(2)}, u32[]{:S(2)}) collective-permute-start(bf16[16,4096]{1,0:T(8,128)(2,1)S(1)} %get-tuple-element.49.x), channel_id=1, source_target_pairs={{0,4},{1,5},{2,6},{3,7},{4,0},{5,1},{6,2},{7,3},{8,12},{9,13},{10,... | collective-permute-start | bytes 393224 | tf_op jit(solution)/shard_map/ppermute | solution.py:24
  83.0 7.0 %collective-permute-start.25 = (bf16[16,4096]{1,0:T(8,128)(2,1)S(1)}, bf16[16,4096]{1,0:T(8,128)(2,1)S(1)}, u32[]{:S(2)}, u32[]{:S(2)}) collective-permute-start(bf16[16,4096]{1,0:T(8,128)(2,1)S(1)} %get-tuple-element.49.x), channel_id=1, source_target_pairs={{0,2},{1,3},{2,0},{3,1},{4,6},{5,7},{6,4},{7,5},{8,10},{9,11},{10,... | collective-permute-start | bytes 393224 | tf_op jit(solution)/shard_map/ppermute | solution.py:24
  88.0 7.2 %collective-permute-start.27 = (bf16[16,4096]{1,0:T(8,128)(2,1)S(1)}, bf16[16,4096]{1,0:T(8,128)(2,1)S(1)}, u32[]{:S(2)}, u32[]{:S(2)}) collective-permute-start(bf16[16,4096]{1,0:T(8,128)(2,1)S(1)} %collective-permute-done.20.x), channel_id=1, source_target_pairs={{0,2},{1,3},{2,0},{3,1},{4,6},{5,7},{6,4},{7,5},{8,10},{9,11},{10,... | collective-permute-start | bytes 393224 | tf_op jit(solution)/shard_map/ppermute | solution.py:24
  89.5 5.0 %collective-permute-start.22 = (bf16[16,4096]{1,0:T(8,128)(2,1)S(1)}, bf16[16,4096]{1,0:T(8,128)(2,1)S(1)}, u32[]{:S(2)}, u32[]{:S(2)}) collective-permute-start(bf16[16,4096]{1,0:T(8,128)(2,1)S(1)} %collective-permute-done.20.x), channel_id=1, source_target_pairs={{0,4},{1,5},{2,6},{3,7},{4,0},{5,1},{6,2},{7,3},{8,12},{9,13},{10,... | collective-permute-start | bytes 393224 | tf_op jit(solution)/shard_map/ppermute | solution.py:24
  89.5 5.7 %collective-permute-start.26 = (bf16[16,4096]{1,0:T(8,128)(2,1)S(1)}, bf16[16,4096]{1,0:T(8,128)(2,1)S(1)}, u32[]{:S(2)}, u32[]{:S(2)}) collective-permute-start(bf16[16,4096]{1,0:T(8,128)(2,1)S(1)} %collective-permute-done.21), channel_id=1, source_target_pairs={{0,2},{1,3},{2,0},{3,1},{4,6},{5,7},{6,4},{7,5},{8,10},{9,11},{10,... | collective-permute-start | bytes 393224 | tf_op jit(solution)/shard_map/ppermute | solution.py:24
  94.5 6.1 %collective-permute-start.23 = (bf16[64,4096]{1,0:T(8,128)(2,1)S(1)}, bf16[64,4096]{1,0:T(8,128)(2,1)S(1)}, u32[]{:S(2)}, u32[]{:S(2)}) collective-permute-start(bf16[64,4096]{1,0:T(8,128)(2,1)S(1)} %pad_maximum_fusion.e0.refs_2_), channel_id=1, source_target_pairs={{0,1},{1,0},{2,3},{3,2},{4,5},{5,4},{6,7},{7,6},{8,9},{9,8},{10,11... | collective-permute-start | bytes 1572872 | tf_op jit(solution)/shard_map/ppermute | solution.py:24
  94.6 5.9 %collective-permute-start.28 = (bf16[16,4096]{1,0:T(8,128)(2,1)S(1)}, bf16[16,4096]{1,0:T(8,128)(2,1)S(1)}, u32[]{:S(2)}, u32[]{:S(2)}) collective-permute-start(bf16[16,4096]{1,0:T(8,128)(2,1)S(1)} %collective-permute-done.22), channel_id=1, source_target_pairs={{0,2},{1,3},{2,0},{3,1},{4,6},{5,7},{6,4},{7,5},{8,10},{9,11},{10,... | collective-permute-start | bytes 393224 | tf_op jit(solution)/shard_map/ppermute | solution.py:24
  100.5 4.1 %collective-permute-start.29 = (bf16[64,4096]{1,0:T(8,128)(2,1)S(1)}, bf16[64,4096]{1,0:T(8,128)(2,1)S(1)}, u32[]{:S(2)}, u32[]{:S(2)}) collective-permute-start(bf16[64,4096]{1,0:T(8,128)(2,1)S(1)} %constant_dynamic-update-slice_fusion.8.e0.refs_4_), channel_id=1, source_target_pairs={{0,1},{1,0},{2,3},{3,2},{4,5},{5,4},{6,7},{7,6},{8,9},{9,8},{10,11... | collective-permute-start | bytes 1572872 | tf_op jit(solution)/shard_map/ppermute | solution.py:24
  103.0 9.2 %collective-permute-start.24 = (bf16[128,1024]{1,0:T(8,128)(2,1)S(1)}, bf16[128,1024]{1,0:T(8,128)(2,1)S(1)}, u32[]{:S(2)}, u32[]{:S(2)}) collective-permute-start(bf16[128,1024]{1,0:T(8,128)(2,1)S(1)} %get-tuple-element.37), channel_id=1, source_target_pairs={{0,16},{16,0},{1,17},{17,1},{2,18},{18,2},{3,19},{19,3},{4,20},{20... | collective-permute-start | bytes 786440 | tf_op jit(solution)/shard_map/ppermute | solution.py:29
  107.1 10.4 %collective-permute-start.30 = (bf16[128,1024]{1,0:T(8,128)(2,1)S(1)}, bf16[128,1024]{1,0:T(8,128)(2,1)S(1)}, u32[]{:S(2)}, u32[]{:S(2)}) collective-permute-start(bf16[128,1024]{1,0:T(8,128)(2,1)S(1)} %get-tuple-element.39), channel_id=1, source_target_pairs={{0,16},{16,0},{1,17},{17,1},{2,18},{18,2},{3,19},{19,3},{4,20},{20... | collective-permute-start | bytes 786440 | tf_op jit(solution)/shard_map/ppermute | solution.py:29
  122.6 10.4 %collective-permute-start.31 = (bf16[64,4096]{1,0:T(8,128)(2,1)S(1)}, bf16[64,4096]{1,0:T(8,128)(2,1)S(1)}, u32[]{:S(2)}, u32[]{:S(2)}) collective-permute-start(bf16[64,4096]{1,0:T(8,128)(2,1)S(1)} %get-tuple-element.41), channel_id=1, source_target_pairs={{0,1},{1,0},{2,3},{3,2},{4,5},{5,4},{6,7},{7,6},{8,9},{9,8},{10,11... | collective-permute-start | bytes 1572872 | tf_op jit(solution)/shard_map/ppermute | solution.py:24
  132.5 2.0 %collective-permute-start.32 = (bf16[64,4096]{1,0:T(8,128)(2,1)S(1)}, bf16[64,4096]{1,0:T(8,128)(2,1)S(1)}, u32[]{:S(2)}, u32[]{:S(2)}) collective-permute-start(bf16[64,4096]{1,0:T(8,128)(2,1)S(1)} %get-tuple-element.43), channel_id=1, source_target_pairs={{0,1},{1,0},{2,3},{3,2},{4,5},{5,4},{6,7},{7,6},{8,9},{9,8},{10,11... | collective-permute-start | bytes 1572872 | tf_op jit(solution)/shard_map/ppermute | solution.py:24
  133.1 14.5 %collective-permute-start.35 = (bf16[16,4096]{1,0:T(8,128)(2,1)S(1)}, bf16[16,4096]{1,0:T(8,128)(2,1)S(1)}, u32[]{:S(2)}, u32[]{:S(2)}) collective-permute-start(bf16[16,4096]{1,0:T(8,128)(2,1)S(1)} %slice.143), channel_id=1, source_target_pairs={{0,4},{1,5},{2,6},{3,7},{4,0},{5,1},{6,2},{7,3},{8,12},{9,13},{10,... | collective-permute-start | bytes 393224 | tf_op jit(solution)/shard_map/ppermute | solution.py:24
  134.7 13.0 %collective-permute-start.36 = (bf16[16,4096]{1,0:T(8,128)(2,1)S(1)}, bf16[16,4096]{1,0:T(8,128)(2,1)S(1)}, u32[]{:S(2)}, u32[]{:S(2)}) collective-permute-start(bf16[16,4096]{1,0:T(8,128)(2,1)S(1)} %get-tuple-element.53), channel_id=1, source_target_pairs={{0,2},{1,3},{2,0},{3,1},{4,6},{5,7},{6,4},{7,5},{8,10},{9,11},{10,... | collective-permute-start | bytes 393224 | tf_op jit(solution)/shard_map/ppermute | solution.py:24
  143.2 19.2 %collective-permute-start.33 = (bf16[16,4096]{1,0:T(8,128)(2,1)S(1)}, bf16[16,4096]{1,0:T(8,128)(2,1)S(1)}, u32[]{:S(2)}, u32[]{:S(2)}) collective-permute-start(bf16[16,4096]{1,0:T(8,128)(2,1)S(1)} %get-tuple-element.51), channel_id=1, source_target_pairs={{0,14},{1,15},{2,12},{3,13},{4,10},{5,11},{6,8},{7,9},{8,6},{9,7},... | collective-permute-start | bytes 393224 | tf_op jit(solution)/shard_map/ppermute | solution.py:24
  145.6 8.7 %collective-permute-start.38 = (bf16[16,4096]{1,0:T(8,128)(2,1)S(1)}, bf16[16,4096]{1,0:T(8,128)(2,1)S(1)}, u32[]{:S(2)}, u32[]{:S(2)}) collective-permute-start(bf16[16,4096]{1,0:T(8,128)(2,1)S(1)} %get-tuple-element.52), channel_id=1, source_target_pairs={{0,2},{1,3},{2,0},{3,1},{4,6},{5,7},{6,4},{7,5},{8,10},{9,11},{10,... | collective-permute-start | bytes 393224 | tf_op jit(solution)/shard_map/ppermute | solution.py:24
  146.2 16.3 %collective-permute-start.34 = (bf16[16,4096]{1,0:T(8,128)(2,1)S(1)}, bf16[16,4096]{1,0:T(8,128)(2,1)S(1)}, u32[]{:S(2)}, u32[]{:S(2)}) collective-permute-start(bf16[16,4096]{1,0:T(8,128)(2,1)S(1)} %get-tuple-element.54), channel_id=1, source_target_pairs={{0,2},{1,3},{2,0},{3,1},{4,6},{5,7},{6,4},{7,5},{8,10},{9,11},{10,... | collective-permute-start | bytes 393224 | tf_op jit(solution)/shard_map/ppermute | solution.py:24
  147.7 14.8 %collective-permute-start.37 = (bf16[16,4096]{1,0:T(8,128)(2,1)S(1)}, bf16[16,4096]{1,0:T(8,128)(2,1)S(1)}, u32[]{:S(2)}, u32[]{:S(2)}) collective-permute-start(bf16[16,4096]{1,0:T(8,128)(2,1)S(1)} %fusion.2), channel_id=1, source_target_pairs={{0,8},{1,9},{2,10},{3,11},{4,12},{5,13},{6,14},{7,15},{8,0},{9,1},... | collective-permute-start | bytes 393224 | tf_op jit(solution)/shard_map/ppermute | solution.py:24
  154.4 8.1 %collective-permute-start.39 = (bf16[16,4096]{1,0:T(8,128)(2,1)S(1)}, bf16[16,4096]{1,0:T(8,128)(2,1)S(1)}, u32[]{:S(2)}, u32[]{:S(2)}) collective-permute-start(bf16[16,4096]{1,0:T(8,128)(2,1)S(1)} %fusion), channel_id=1, source_target_pairs={{0,4},{1,5},{2,6},{3,7},{4,0},{5,1},{6,2},{7,3},{8,12},{9,13},{10,... | collective-permute-start | bytes 393224 | tf_op jit(solution)/shard_map/ppermute | solution.py:24

commit v2 on v1

--- a/solution.py
+++ b/solution.py
@@ -57,10 +57,6 @@
     return pltpu.with_memory_space_constraint(a, pltpu.VMEM)
 
 
-def whole(a):
-    return pl.BlockSpec(a.shape, lambda i: (0,) * a.ndim)
-
-
 def load_body(w, m, out, sems):
     n = sems.shape[0]
     rows = w.shape[0] // n
@@ -96,20 +92,20 @@
     return call(tick_body, [pltpu.VMEM((8, BLOCK), F32)], (x,), 0, in_specs=[HB], limit=1, effects=True)
 
 
-def gate_up_body(x0, x1, ge, ue, own, send):
+def project_body(x0, x1, *refs):
+    ws, own, send = refs[:-2], refs[-2], refs[-1]
     x = jnp.concatenate([x0[...], x1[...]], axis=0)
-    f = ge.shape[1]
-    for w, off in ((ge, 0), (ue, f)):
+    f = ws[0].shape[1]
+    for i, w in enumerate(ws):
         part = jnp.dot(x, w[...], preferred_element_type=F32)
-        own[:, off : off + f] = part
-        send[:, off : off + f] = part.astype(BF16)
-
-
-def gate_up(x0, x1, ge, ue):
-    d, f = ge.shape
-    m = 2 * x0.shape[0]
-    outs = [sds((m, 2 * f), F32), sds((m, 2 * f), BF16)]
-    return call(gate_up_body, outs, (x0, x1, vm(ge), vm(ue)), 4 * m * d * f)
+        own[:, i * f : (i + 1) * f] = part
+        send[:, i * f : (i + 1) * f] = part.astype(BF16)
+
+
+def project(x0, x1, ws):
+    d, f = ws[0].shape
+    m, n = 2 * x0.shape[0], len(ws) * f
+    return call(project_body, [sds((m, n), F32), sds((m, n), BF16)], (x0, x1, *map(vm, ws)), 2 * m * d * n)
 
 
 def total(own, recvs):
@@ -119,15 +115,21 @@
     return out
 
 
+def taken(refs, counts):
+    values = []
+    for n in counts:
+        values.append(total(refs[0], refs[1:n]))
+        refs = refs[n:]
+    return jnp.concatenate(values, axis=1), refs
+
+
 def columns(d, n):
     return [slice(c, min(c + n, d)) for c in range(0, d, n)]
 
 
-def down_body(n, *refs):
-    act, recvs = refs[0], refs[1 : 1 + n]
-    de, hidden, own, send = refs[1 + n :]
+def down_body(counts, *refs):
+    both, (de, hidden, own, send) = taken(refs, counts)
     f, d = de.shape
-    both = total(act, recvs)
     gate, up = both[:, :f], both[:, f:]
     h = (gate * jax.nn.sigmoid(gate) * up).astype(BF16)
     hidden[...] = h
@@ -138,11 +140,12 @@
         send[:, c] = part[half:].astype(BF16)
 
 
-def down(act, recvs, de):
+def down(parts, de):
     f, d = de.shape
-    m = act.shape[0]
+    m = parts[0][0].shape[0]
     outs = [sds((m, f), BF16), sds((m // 2, d), F32), sds((m // 2, d), BF16)]
-    return call(functools.partial(down_body, len(recvs)), outs, (act, *recvs, vm(de)), 2 * m * d * f)
+    args = [a for p in parts for a in p] + [vm(de)]
+    return call(functools.partial(down_body, [len(p) for p in parts]), outs, args, 2 * m * d * f)
 
 
 def hidden_grad_body(e0, e1, de, own, send):
@@ -167,23 +170,17 @@
         row += p.shape[0]
 
 
-def wgrad_block(ls, right, c, mask, factor, store):
-    left = jnp.concatenate([l[:, c] for l in ls], axis=0)
-    w = lax.dot_general(left, right[...], BY_ROWS, preferred_element_type=F32)
-    for k in range((c.stop - c.start) // BLOCK):
-        rows = slice(k * BLOCK, (k + 1) * BLOCK)
-        store(rows, w[rows, :] * (mask[c.start // BLOCK + k] * factor))
-
-
-def input_grad_body(groups, n, *refs):
-    acts, refs = [refs[g * (1 + n) : (g + 1) * (1 + n)] for g in range(groups)], refs[groups * (1 + n) :]
-    hids, refs = [refs[g * (1 + n) : (g + 1) * (1 + n)] for g in range(groups)], refs[groups * (1 + n) :]
+def input_grad_body(acts, hids, *refs):
+    values = []
+    for counts in (*acts, *hids):
+        value, refs = taken(refs, counts)
+        values.append(value)
+    groups = len(acts)
     ge, ue, gg_ref, ug_ref = refs[:4]
     owns, sends = refs[4 : 4 + groups], refs[4 + groups :]
     d, f = ge.shape
     m = gg_ref.shape[0] // groups
-    for g, (act, hid) in enumerate(zip(acts, hids)):
-        both, hg = total(act[0], act[1:]), total(hid[0], hid[1:])
+    for g, (both, hg) in enumerate(zip(values[:groups], values[groups:])):
         gate, up = both[:, :f], both[:, f:]
         sigma = jax.nn.sigmoid(gate)
         swish = gate * sigma
@@ -200,54 +197,78 @@
 
 def input_grad(acts, hids, ge, ue):
     d, f = ge.shape
-    groups, m, n = len(acts), acts[0][0].shape[0], len(acts[0][1])
+    groups, m = len(acts), acts[0][0][0].shape[0]
     outs = [sds((groups * m, f), BF16)] * 2 + [sds((m // 2, d), F32)] * groups + [sds((m // 2, d), BF16)] * groups
-    args = [a for own, recvs in (*acts, *hids) for a in (own, *recvs)] + [vm(ge), vm(ue)]
-    gg, ug, *rest = call(functools.partial(input_grad_body, groups, n), outs, args, 4 * groups * m * d * f, limit=12)
+    args = [a for parts in (*acts, *hids) for p in parts for a in p] + [vm(ge), vm(ue)]
+    counts = [[[len(p) for p in parts] for parts in group] for group in (acts, hids)]
+    gg, ug, *rest = call(
+        functools.partial(input_grad_body, *counts), outs, args, 4 * groups * m * d * f,
+        limit=max(8, groups * m // 64),
+    )
     return gg, ug, list(zip(rest[:groups], rest[groups:]))
 
 
-def wgrad_body(nl, nr, factor, aliased, *refs):
-    ls, rs, mask = refs[:nl], refs[nl : nl + nr], refs[nl + nr]
-    out, right = refs[nl + nr + 1 + aliased :]
+def wgrad_body(nl, jobs, factor, aliased, *refs):
+    ls, refs = refs[:nl], refs[nl:]
+    work = []
+    for nr in jobs:
+        work.append((refs[:nr], refs[nr]))
+        refs = refs[nr + 1 :]
+    refs = refs[aliased:]
+    outs, rights = refs[: len(jobs)], refs[len(jobs) :]
 
     @pl.when(pl.program_id(0) == 0)
     def _():
-        stack(right, rs)
-
-    def store(rows, value):
-        out[rows, :] = value
-
-    wgrad_block(ls, right, slice(0, out.shape[0]), mask, factor, store)
-
-
-def wgrad(ls, rs, mask, factor, size, first, count, prev):
-    a, b = ls[0].shape[1], rs[0].shape[1]
-    m = sum(l.shape[0] for l in ls)
-    specs = [pl.BlockSpec((l.shape[0], size), lambda i: (0, first + i)) for l in ls] + [whole(r) for r in rs]
-    specs.append(pl.BlockSpec((size // BLOCK, 1, b), lambda i: (first + i, 0, 0)))
-    args = (*ls, *rs, mask)
-    if prev is not None:
-        args, specs = (*args, prev), specs + [HB]
+        for (rs, _), right in zip(work, rights):
+            stack(right, rs)
+
+    left = jnp.concatenate([l[...] for l in ls], axis=0)
+    for (_, mask), out, right in zip(work, outs, rights):
+        w = lax.dot_general(left, right[...], BY_ROWS, preferred_element_type=F32)
+        for k in range(out.shape[0] // BLOCK):
+            rows = slice(k * BLOCK, (k + 1) * BLOCK)
+            out[rows, :] = w[rows, :] * (mask[k] * factor)
+
+
+def wgrad(ls, jobs, factor, size, first, count, prev):
+    a, b = ls[0].shape[1], jobs[0][0][0].shape[1]
+    m, n = sum(l.shape[0] for l in ls), len(jobs)
+    specs = [pl.BlockSpec((l.shape[0], size), lambda i: (0, first + i)) for l in ls]
+    args = list(ls)
+    for rs, mask in jobs:
+        args += [*rs, mask]
+        specs += [VM for r in rs] + [pl.BlockSpec((size // BLOCK, 1, b), lambda i: (first + i, 0, 0))]
+    aliases = {}
+    for i, p in enumerate(prev or ()):
+        aliases[len(args)] = i
+        args.append(p)
+        specs.append(HB)
     return call(
-        functools.partial(wgrad_body, len(ls), len(rs), factor, int(prev is not None)), [sds((a, b), F32)],
-        args, 2 * m * size * count * b, in_specs=specs,
-        out_specs=[pl.BlockSpec((size, b), lambda i: (first + i, 0))],
-        grid=(count,), scratch=[pltpu.VMEM((m, b), BF16)], limit=16,
-        aliases={} if prev is None else {len(args) - 1: 0},
-    )[0]
-
-
-def gather(shard, zs, xs, ticks):
+        functools.partial(wgrad_body, len(ls), [len(rs) for rs, _ in jobs], factor, len(aliases)),
+        [sds((a, b), F32)] * n, tuple(args), 2 * m * size * count * b * n, in_specs=specs,
+        out_specs=[pl.BlockSpec((size, b), lambda i: (first + i, 0))] * n,
+        grid=(count,), scratch=[pltpu.VMEM((m, b), BF16)] * n, limit=12, aliases=aliases,
+    )
+
+
+def gather(shard, zs, xs, ticks, split):
     column = [shard] + [swap(shard, "hid", z) for z in zs[:2]]
     if zs:
         column.append(swap(column[2], "hid", zs[0]))
     groups = [column] + [[swap(p, "hid", x) for p in column] for x in xs]
     if ticks:
-        tick(shard)
+        tick(column[1])
         tick(column[2])
-    halves = [jnp.concatenate(g, axis=0) for g in groups]
-    return [(h, swap(h, "hid", 1)) for h in halves]
+    out = []
+    for i, g in enumerate(groups):
+        n = len(g) // (split if i == 0 and len(g) % split == 0 else 1)
+        rows = [jnp.concatenate(g[j : j + n], axis=0) for j in range(0, len(g), n)]
+        out.append([(r, swap(r, "hid", 1)) for r in rows])
+    return out
+
+
+def rows_of(groups):
+    return [part[c] for parts in groups for c in (0, 1) for part in parts]
 
 
 def scatter(parts, zs, xs, ticks):
@@ -292,31 +313,34 @@
     gm, um, dm = wide(block_mask[0]), wide(block_mask[1]), wide(block_mask[2].T)
     ge, ue, de = load(gw, gm), load(uw, um), load(dw, dm)
 
-    inputs = gather(student_in, zs, xs, False)
+    inputs = gather(student_in, zs, xs, False, 1)
     acts = []
-    for x0, x1 in inputs:
-        own, send = gate_up(x0, x1, ge, ue)
-        acts.append((own, shifts(send)))
+    for ((x0, x1),) in inputs:
+        group = []
+        for ws in ([ge, ue],):
+            own, send = project(x0, x1, ws)
+            group.append((own, *shifts(send)))
+        acts.append(group)
     hiddens, parts = [], []
-    for own, recvs in acts:
-        h, o, s = down(own, recvs, de)
+    for group in acts:
+        h, o, s = down(group, de)
         hiddens.append(h)
         parts.append((o, s))
     output_sum = scatter(parts, zs, xs, True)
     error = (output_sum - target_delta.astype(F32)).astype(BF16)
-    errors = gather(error, zs, xs, True)
+    errors = gather(error, zs, xs, True, 1)
     hgs = []
-    for e0, e1 in errors:
+    for ((e0, e1),) in errors:
         own, send = hidden_grad(e0, e1, de)
-        hgs.append((own, shifts(send)))
-    all_in = [p for x in inputs for p in x]
-    all_err = [p for e in errors for p in e]
+        hgs.append([(own, *shifts(send))])
+    all_in, all_err = rows_of(inputs), rows_of(errors)
     d, f = gw.shape
-    dsize, gsize = BLOCK, min(512, d)
-    down_w = wgrad(hiddens, all_err, dm, factor, dsize, 0, f // dsize, None)
+    (down_w,) = wgrad(hiddens, [(all_err, dm)], factor, BLOCK, 0, f // BLOCK, None)
     gg, ug, parts = input_grad(acts, hgs, ge, ue)
-    gate_w = wgrad(all_in, [gg], gm, factor, gsize, 0, d // gsize, None)
-    up_w = wgrad(all_in, [ug], um, factor, gsize, 0, d // gsize, None)
+    jobs, size = [([gg], gm), ([ug], um)], min(256, d // 2)
+    steps = d // size // 2
+    early = wgrad(all_in, jobs, factor, size, 0, steps, None)
+    gate_w, up_w = wgrad(all_in, jobs, factor, size, steps, steps, early)
     grad = scatter(parts, zs, xs, False)
     return (output_sum.astype(BF16), grad.astype(BF16), gate_w, up_w, down_w)
 

time: 163 us -> 158 us (0.969)
  waiting for transfers between devices: 69.2 us -> 55 us
  starting transfers between devices: 34.3 us -> 44.1 us
    ppermute x36, waiting for transfers between devices: 43.7 us -> 29.4 us  [swap(): return lax.ppermute(x, axis, [(i, i ^ offset) for i in range(n)])]
    ppermute x36, starting transfers between devices: 29.9 us -> 39.8 us  [swap(): return lax.ppermute(x, axis, [(i, i ^ offset) for i in range(n)])]
  transfers between devices with their start and end apart: 40 -> 40, of which waited for: 19 -> 18; matrix products, arithmetic and copies ran while one was open for 2% -> 2% of each run, Pallas kernels for 30% -> 31%
where the time goes in v2:
time: 158 us
  waiting for transfers between devices  55 us (35%)
  Pallas kernels  53.2 us (34%)
  starting transfers between devices  44.1 us (28%)
  other arithmetic  2.79 us (2%)
  local copies, waits for them, and re-layouts  1.58 us (1%)
    pallas_call x16, Pallas kernels, call(): pl.pallas_call(body, grid=grid, in_specs=in_specs or [VM] * len(args), ou...  53.2 us
    ppermute x36, starting transfers between devices, swap(): return lax.ppermute(x, axis, [(i, i ^ offset) for i in range(n)])  39.8 us
    ppermute x36, waiting for transfers between devices, swap(): return lax.ppermute(x, axis, [(i, i ^ offset) for i in range(n)])  29.4 us
    ppermute x4, waiting for transfers between devices, shifts(): lax.ppermute(x, 'tok', [(i, (i + d) % n) for i in range(n)])  25.6 us
    ppermute x4, starting transfers between devices, shifts(): lax.ppermute(x, 'tok', [(i, (i + d) % n) for i in range(n)])  4.31 us
  transfers between devices with their start and end apart: 40, of which 18 were waited for; matrix products, arithmetic and copies ran while one was open for 2% of the time, Pallas kernels for 31%

profile of v2, /device:TPU:0, one launch (start us, length us, event | category | flops | bytes accessed | tf_op | source)
XLA Modules:
  0.0 157.7 jit_solution(789155320766403362)
XLA Ops:
  0.6 3.0 %collective-permute-start.7 = (bf16[16,4096]{1,0:T(8,128)(2,1)}, bf16[16,4096]{1,0:T(8,128)(2,1)S(1)}, u32[]{:S(2)}, u32[]{:S(2)}) collective-permute-start(bf16[16,4096]{1,0:T(8,128)(2,1)} %param.6), channel_id=1, source_target_pairs={{0,2},{1,3},{2,0},{3,1},{4,6},{5,7},{6,4},{7,5},{8,10},{9,11},{10,... | collective-permute-start | bytes 393224 | tf_op jit(solution)/shard_map/ppermute | solution.py:24
  3.7 1.6 collective-permute-start
  5.2 2.6 %collective-permute-start.1 = (bf16[16,4096]{1,0:T(8,128)(2,1)}, bf16[16,4096]{1,0:T(8,128)(2,1)S(1)}, u32[]{:S(2)}, u32[]{:S(2)}) collective-permute-start(bf16[16,4096]{1,0:T(8,128)(2,1)} %param.6), channel_id=1, source_target_pairs={{0,8},{1,9},{2,10},{3,11},{4,12},{5,13},{6,14},{7,15},{8,0},{9,1},... | collective-permute-start | bytes 393224 | tf_op jit(solution)/shard_map/ppermute | solution.py:24
  7.8 0.9 constant_dynamic-update-slice_fusion.3
  8.8 0.7 convert_bitcast_fusion
  9.8 3.7 %shard_map.101.refs_0_.refs_8_ = bf16[4096,1024]{1,0:T(8,128)(2,1)S(1)} custom-call(bf16[4096,1024]{1,0:T(8,128)(2,1)} %w.3, f32[32,1,1024]{2,1,0:T(1,128)S(1)} %bitcast.11), custom_call_target="tpu_custom_call" | custom-call | bytes 16908288 | tf_op jit(solution)/shard_map/pallas_call | solution.py:39
  13.5 3.7 %shard_map.102.refs_1_.refs_9_ = bf16[4096,1024]{1,0:T(8,128)(2,1)S(1)} custom-call(bf16[4096,1024]{1,0:T(8,128)(2,1)} %w.4, f32[32,1,1024]{2,1,0:T(1,128)S(1)} %bitcast.14), custom_call_target="tpu_custom_call" | custom-call | bytes 16908288 | tf_op jit(solution)/shard_map/pallas_call | solution.py:39
  17.3 0.6 collective-permute-start.9
  17.9 0.4 collective-permute-start.2
  18.3 1.6 collective-permute-start.8
  19.9 2.9 %collective-permute-done.2 = bf16[16,4096]{1,0:T(8,128)(2,1)S(1)} collective-permute-done((bf16[16,4096]{1,0:T(8,128)(2,1)S(1)}, bf16[16,4096]{1,0:T(8,128)(2,1)S(1)}, u32[]{:S(2)}, u32[]{:S(2)}) %collective-permute-start.2) | collective-permute-done | bytes 131104 | tf_op jit(solution)/shard_map/ppermute | solution.py:24
  22.9 1.6 collective-permute-start.10
  24.6 4.2 %collective-permute-done.10 = bf16[16,4096]{1,0:T(8,128)(2,1)S(1)} collective-permute-done((bf16[16,4096]{1,0:T(8,128)(2,1)S(1)}, bf16[16,4096]{1,0:T(8,128)(2,1)S(1)}, u32[]{:S(2)}, u32[]{:S(2)}) %collective-permute-start.10) | collective-permute-done | bytes 131104 | tf_op jit(solution)/shard_map/ppermute | solution.py:24
  28.9 2.3 %shard_map.103 = (f32[128,2048]{1,0:T(8,128)S(1)}, bf16[128,2048]{1,0:T(8,128)(2,1)S(1)}) custom-call(bf16[64,4096]{1,0:T(8,128)(2,1)S(1)} %constant_dynamic-update-slice_fusion.x0.refs_0_, bf16[64,4096]{1,0:T(8,128)(2,1)S(1)} %collective-permute-done.3.x1.refs_1_, bf16[4096,1024]{1,0:T(8,128)(2,1)S(1)} %shard_map.101.refs_0_.refs_8_, ...), custom_call_target="tpu_custom_call" | custom-call | flops 2147483648 | bytes 19398656 | tf_op jit(solution)/shard_map/pallas_call | solution.py:39
  31.3 1.6 %collective-permute-start.4 = (bf16[128,2048]{1,0:T(8,128)(2,1)S(1)}, bf16[128,2048]{1,0:T(8,128)(2,1)S(1)}, u32[]{:S(2)}, u32[]{:S(2)}) collective-permute-start(bf16[128,2048]{1,0:T(8,128)(2,1)S(1)} %get-tuple-element.32), channel_id=1, source_target_pairs={{0,16},{16,0},{1,17},{17,1},{2,18},{18,2},{3,19},{19,3},{4,20},{20... | collective-permute-start | bytes 1572872 | tf_op jit(solution)/shard_map/ppermute | solution.py:29
  32.9 3.8 %shard_map.104.refs_2_.de = bf16[1024,4096]{1,0:T(8,128)(2,1)S(1)} custom-call(bf16[1024,4096]{1,0:T(8,128)(2,1)} %w.5, f32[8,1,4096]{2,1,0:T(1,128)S(1)} %bitcast.17), custom_call_target="tpu_custom_call" | custom-call | bytes 16908288 | tf_op jit(solution)/shard_map/pallas_call | solution.py:39
  36.8 2.3 %shard_map.106 = (f32[128,2048]{1,0:T(8,128)S(1)}, bf16[128,2048]{1,0:T(8,128)(2,1)S(1)}) custom-call(bf16[64,4096]{1,0:T(8,128)(2,1)S(1)} %constant_dynamic-update-slice_fusion.4.x0.refs_2_, bf16[64,4096]{1,0:T(8,128)(2,1)S(1)} %collective-permute-done.11.x1.refs_3_, bf16[4096,1024]{1,0:T(8,128)(2,1)S(1)} %shard_map.101.refs_0_.refs_8_, ...), custom_call_target="tpu_custom_call" | custom-call | flops 2147483648 | bytes 19398656 | tf_op jit(solution)/shard_map/pallas_call | solution.py:39
  39.2 0.6 collective-permute-start.12
  39.7 6.4 %collective-permute-done.4.refs_1_ = bf16[128,2048]{1,0:T(8,128)(2,1)S(1)} collective-permute-done((bf16[128,2048]{1,0:T(8,128)(2,1)S(1)}, bf16[128,2048]{1,0:T(8,128)(2,1)S(1)}, u32[]{:S(2)}, u32[]{:S(2)}) %collective-permute-start.4) | collective-permute-done | bytes 524320 | tf_op jit(solution)/shard_map/ppermute | solution.py:29
  46.1 1.3 shard_map.105
  47.5 9.4 %collective-permute-done.12.refs_1_.refs_3_ = bf16[128,2048]{1,0:T(8,128)(2,1)S(1)} collective-permute-done((bf16[128,2048]{1,0:T(8,128)(2,1)S(1)}, bf16[128,2048]{1,0:T(8,128)(2,1)S(1)}, u32[]{:S(2)}, u32[]{:S(2)}) %collective-permute-start.12) | collective-permute-done | bytes 524320 | tf_op jit(solution)/shard_map/ppermute | solution.py:29
  56.9 1.3 shard_map.107
  58.4 1.8 %collective-permute-done.13 = bf16[64,4096]{1,0:T(8,128)(2,1)S(1)} collective-permute-done((bf16[64,4096]{1,0:T(8,128)(2,1)S(1)}, bf16[64,4096]{1,0:T(8,128)(2,1)S(1)}, u32[]{:S(2)}, u32[]{:S(2)}) %collective-permute-start.13) | collective-permute-done | bytes 524320 | tf_op jit(solution)/shard_map/ppermute | solution.py:24
  60.3 1.6 collective-permute-start.18
  62.3 0.5 collective-permute-start.14
  62.9 1.5 collective-permute-start.16
  64.4 1.3 collective-permute-start.15
  65.7 1.1 collective-permute-done.18
  67.1 5.2 %collective-permute-done.14 = bf16[16,4096]{1,0:T(8,128)(2,1)S(1)} collective-permute-done((bf16[16,4096]{1,0:T(8,128)(2,1)S(1)}, bf16[16,4096]{1,0:T(8,128)(2,1)S(1)}, u32[]{:S(2)}, u32[]{:S(2)}) %collective-permute-start.14) | collective-permute-done | bytes 131104 | tf_op jit(solution)/shard_map/ppermute | solution.py:24
  72.6 1.7 %collective-permute-done.16 = bf16[16,4096]{1,0:T(8,128)(2,1)S(1)} collective-permute-done((bf16[16,4096]{1,0:T(8,128)(2,1)S(1)}, bf16[16,4096]{1,0:T(8,128)(2,1)S(1)}, u32[]{:S(2)}, u32[]{:S(2)}) %collective-permute-start.16) | collective-permute-done | bytes 131104 | tf_op jit(solution)/shard_map/ppermute | solution.py:24
  74.4 4.5 %collective-permute-done.19 = bf16[16,4096]{1,0:T(8,128)(2,1)S(1)} collective-permute-done((bf16[16,4096]{1,0:T(8,128)(2,1)S(1)}, bf16[16,4096]{1,0:T(8,128)(2,1)S(1)}, u32[]{:S(2)}, u32[]{:S(2)}) %collective-permute-start.19) | collective-permute-done | bytes 131104 | tf_op jit(solution)/shard_map/ppermute | solution.py:24
  78.9 0.8 subtract_convert_fusion
  79.7 1.1 collective-permute-start.21
  80.8 1.4 collective-permute-start.25
  82.1 3.5 %collective-permute-start.20 = (bf16[16,4096]{1,0:T(8,128)(2,1)S(1)}, bf16[16,4096]{1,0:T(8,128)(2,1)S(1)}, u32[]{:S(2)}, u32[]{:S(2)}) collective-permute-start(bf16[16,4096]{1,0:T(8,128)(2,1)S(1)} %get-tuple-element.57), channel_id=1, source_target_pairs={{0,4},{1,5},{2,6},{3,7},{4,0},{5,1},{6,2},{7,3},{8,12},{9,13},{10,... | collective-permute-start | bytes 393224 | tf_op jit(solution)/shard_map/ppermute | solution.py:24
  85.6 2.5 %collective-permute-start.22 = (bf16[16,4096]{1,0:T(8,128)(2,1)S(1)}, bf16[16,4096]{1,0:T(8,128)(2,1)S(1)}, u32[]{:S(2)}, u32[]{:S(2)}) collective-permute-start(bf16[16,4096]{1,0:T(8,128)(2,1)S(1)} %collective-permute-done.21.x), channel_id=1, source_target_pairs={{0,4},{1,5},{2,6},{3,7},{4,0},{5,1},{6,2},{7,3},{8,12},{9,13},{10,... | collective-permute-start | bytes 393224 | tf_op jit(solution)/shard_map/ppermute | solution.py:24
  88.1 1.6 collective-permute-start.27
  89.7 0.5 collective-permute-start.26
  90.3 0.8 collective-permute-done.22
  91.2 1.6 %collective-permute-start.28 = (bf16[16,4096]{1,0:T(8,128)(2,1)S(1)}, bf16[16,4096]{1,0:T(8,128)(2,1)S(1)}, u32[]{:S(2)}, u32[]{:S(2)}) collective-permute-start(bf16[16,4096]{1,0:T(8,128)(2,1)S(1)} %collective-permute-done.22), channel_id=1, source_target_pairs={{0,2},{1,3},{2,0},{3,1},{4,6},{5,7},{6,4},{7,5},{8,10},{9,11},{10,... | collective-permute-start | bytes 393224 | tf_op jit(solution)/shard_map/ppermute | solution.py:24
  92.8 2.4 %collective-permute-done.26 = bf16[16,4096]{1,0:T(8,128)(2,1)S(1)} collective-permute-done((bf16[16,4096]{1,0:T(8,128)(2,1)S(1)}, bf16[16,4096]{1,0:T(8,128)(2,1)S(1)}, u32[]{:S(2)}, u32[]{:S(2)}) %collective-permute-start.26) | collective-permute-done | bytes 131104 | tf_op jit(solution)/shard_map/ppermute | solution.py:24
  95.3 2.3 %collective-permute-done.28 = bf16[16,4096]{1,0:T(8,128)(2,1)S(1)} collective-permute-done((bf16[16,4096]{1,0:T(8,128)(2,1)S(1)}, bf16[16,4096]{1,0:T(8,128)(2,1)S(1)}, u32[]{:S(2)}, u32[]{:S(2)}) %collective-permute-start.28) | collective-permute-done | bytes 131104 | tf_op jit(solution)/shard_map/ppermute | solution.py:24
  97.7 2.4 %shard_map.111 = (f32[128,1024]{1,0:T(8,128)S(1)}, bf16[128,1024]{1,0:T(8,128)(2,1)S(1)}) custom-call(bf16[64,4096]{1,0:T(8,128)(2,1)S(1)} %pad_maximum_fusion.e0.refs_2_, bf16[64,4096]{1,0:T(8,128)(2,1)S(1)} %collective-permute-done.23.e1.refs_3_, bf16[1024,4096]{1,0:T(8,128)(2,1)S(1)} %shard_map.104.refs_2_.de), custom_call_target="tpu_custom_call" | custom-call | flops 1073741824 | bytes 10223616 | tf_op jit(solution)/shard_map/pallas_call | solution.py:39
  100.1 1.6 %collective-permute-start.24 = (bf16[128,1024]{1,0:T(8,128)(2,1)S(1)}, bf16[128,1024]{1,0:T(8,128)(2,1)S(1)}, u32[]{:S(2)}, u32[]{:S(2)}) collective-permute-start(bf16[128,1024]{1,0:T(8,128)(2,1)S(1)} %get-tuple-element.41), channel_id=1, source_target_pairs={{0,16},{16,0},{1,17},{17,1},{2,18},{18,2},{3,19},{19,3},{4,20},{20... | collective-permute-start | bytes 786440 | tf_op jit(solution)/shard_map/ppermute | solution.py:29
  101.7 2.4 %shard_map.112 = (f32[128,1024]{1,0:T(8,128)S(1)}, bf16[128,1024]{1,0:T(8,128)(2,1)S(1)}) custom-call(bf16[64,4096]{1,0:T(8,128)(2,1)S(1)} %constant_dynamic-update-slice_fusion.8.e0.refs_4_, bf16[64,4096]{1,0:T(8,128)(2,1)S(1)} %collective-permute-done.29.e1.refs_5_, bf16[1024,4096]{1,0:T(8,128)(2,1)S(1)} %shard_map.104.refs_2_.de), custom_call_target="tpu_custom_call" | custom-call | flops 1073741824 | bytes 10223616 | tf_op jit(solution)/shard_map/pallas_call | solution.py:39
  104.1 0.6 collective-permute-start.30
  104.7 4.7 %collective-permute-done.24.refs_5_ = bf16[128,1024]{1,0:T(8,128)(2,1)S(1)} collective-permute-done((bf16[128,1024]{1,0:T(8,128)(2,1)S(1)}, bf16[128,1024]{1,0:T(8,128)(2,1)S(1)}, u32[]{:S(2)}, u32[]{:S(2)}) %collective-permute-start.24) | collective-permute-done | bytes 262176 | tf_op jit(solution)/shard_map/ppermute | solution.py:29
  109.3 5.1 %collective-permute-done.30.refs_7_ = bf16[128,1024]{1,0:T(8,128)(2,1)S(1)} collective-permute-done((bf16[128,1024]{1,0:T(8,128)(2,1)S(1)}, bf16[128,1024]{1,0:T(8,128)(2,1)S(1)}, u32[]{:S(2)}, u32[]{:S(2)}) %collective-permute-start.30) | collective-permute-done | bytes 262176 | tf_op jit(solution)/shard_map/ppermute | solution.py:29
  114.5 5.1 %shard_map.113 = (bf16[256,1024]{1,0:T(8,128)(2,1)S(1)}, bf16[256,1024]{1,0:T(8,128)(2,1)S(1)}, f32[64,4096]{1,0:T(8,128)S(1)}, f32[64,4096]{1,0:T(8,128)S(1)}, ...) custom-call(f32[128,2048]{1,0:T(8,128)S(1)} %get-tuple-element.31.refs_0_, ...), custom_call_target="tpu_custom_call" | custom-call | flops 4294967296 | bytes 25690112 | tf_op jit(solution)/shard_map/pallas_call | solution.py:39
  119.7 0.6 shard_map.108
  120.3 0.6 shard_map.109
  120.9 0.6 shard_map.110
  121.5 8.1 %shard_map.116 = f32[1024,4096]{1,0:T(8,128)} custom-call(bf16[128,1024]{1,0:T(8,128)(2,1)S(1)} %get-tuple-element.55.refs_0_, bf16[128,1024]{1,0:T(8,128)(2,1)S(1)} %get-tuple-element.56.refs_1_, bf16[64,4096]{1,0:T(8,128)(2,1)S(1)} %pad_maximum_fusion.e0.refs_2_, bf16[64,4096]{1,0:T(8,128)(2,1)S(1)} %collective-permute-done.23.e1.refs_3_, ...), custom_call_target="tpu_custom_call" | custom-call | flops 2147483648 | bytes 19529728 | tf_op jit(solution)/shard_map/pallas_call | solution.py:39
  129.6 0.5 collective-permute-start.31
  130.2 1.4 collective-permute-start.36
  131.7 1.9 %collective-permute-start.35 = (bf16[16,4096]{1,0:T(8,128)(2,1)S(1)}, bf16[16,4096]{1,0:T(8,128)(2,1)S(1)}, u32[]{:S(2)}, u32[]{:S(2)}) collective-permute-start(bf16[16,4096]{1,0:T(8,128)(2,1)S(1)} %slice.143), channel_id=1, source_target_pairs={{0,4},{1,5},{2,6},{3,7},{4,0},{5,1},{6,2},{7,3},{8,12},{9,13},{10,... | collective-permute-start | bytes 393224 | tf_op jit(solution)/shard_map/ppermute | solution.py:24
  133.6 7.4 %shard_map.114 = (f32[4096,1024]{1,0:T(8,128)}, f32[4096,1024]{1,0:T(8,128)}) custom-call(bf16[64,4096]{1,0:T(8,128)(2,1)S(1)} %constant_dynamic-update-slice_fusion.x0.refs_0_, bf16[64,4096]{1,0:T(8,128)(2,1)S(1)} %collective-permute-done.3.x1.refs_1_, bf16[64,4096]{1,0:T(8,128)(2,1)S(1)} %constant_dynamic-update-slice_fusion.4.x0.refs_2_, ...), custom_call_target="tpu_custom_call" | custom-call | flops 2147483648 | bytes 36962304 | tf_op jit(solution)/shard_map/pallas_call | solution.py:39
  141.0 1.3 collective-permute-start.38
  142.3 0.7 collective-permute-start.34
  143.0 2.3 %collective-permute-start.33 = (bf16[16,4096]{1,0:T(8,128)(2,1)S(1)}, bf16[16,4096]{1,0:T(8,128)(2,1)S(1)}, u32[]{:S(2)}, u32[]{:S(2)}) collective-permute-start(bf16[16,4096]{1,0:T(8,128)(2,1)S(1)} %get-tuple-element.59), channel_id=1, source_target_pairs={{0,14},{1,15},{2,12},{3,13},{4,10},{5,11},{6,8},{7,9},{8,6},{9,7},... | collective-permute-start | bytes 393224 | tf_op jit(solution)/shard_map/ppermute | solution.py:24
  145.6 1.8 %collective-permute-done.38 = bf16[16,4096]{1,0:T(8,128)(2,1)S(1)} collective-permute-done((bf16[16,4096]{1,0:T(8,128)(2,1)S(1)}, bf16[16,4096]{1,0:T(8,128)(2,1)S(1)}, u32[]{:S(2)}, u32[]{:S(2)}) %collective-permute-start.38) | collective-permute-done | bytes 131104 | tf_op jit(solution)/shard_map/ppermute | solution.py:24
  147.4 1.9 %collective-permute-start.39 = (bf16[16,4096]{1,0:T(8,128)(2,1)S(1)}, bf16[16,4096]{1,0:T(8,128)(2,1)S(1)}, u32[]{:S(2)}, u32[]{:S(2)}) collective-permute-start(bf16[16,4096]{1,0:T(8,128)(2,1)S(1)} %fusion), channel_id=1, source_target_pairs={{0,4},{1,5},{2,6},{3,7},{4,0},{5,1},{6,2},{7,3},{8,12},{9,13},{10,... | collective-permute-start | bytes 393224 | tf_op jit(solution)/shard_map/ppermute | solution.py:24
  149.4 7.4 %shard_map.115 = (f32[4096,1024]{1,0:T(8,128)}, f32[4096,1024]{1,0:T(8,128)}) custom-call(bf16[64,4096]{1,0:T(8,128)(2,1)S(1)} %constant_dynamic-update-slice_fusion.x0.refs_0_, bf16[64,4096]{1,0:T(8,128)(2,1)S(1)} %collective-permute-done.3.x1.refs_1_, ...), custom_call_target="tpu_custom_call", output_to_operand_aliasing={{0}: (8, {}), {1}: (9, {})} | custom-call | flops 2147483648 | bytes 70516736 | tf_op jit(solution)/shard_map/pallas_call | solution.py:39
  157.0 0.7 fusion.6
  (69 shorter events, 3.1 us)
Async XLA Ops:
  0.6 17.7 %collective-permute-start.7 = (bf16[16,4096]{1,0:T(8,128)(2,1)}, bf16[16,4096]{1,0:T(8,128)(2,1)S(1)}, u32[]{:S(2)}, u32[]{:S(2)}) collective-permute-start(bf16[16,4096]{1,0:T(8,128)(2,1)} %param.6), channel_id=1, source_target_pairs={{0,2},{1,3},{2,0},{3,1},{4,6},{5,7},{6,4},{7,5},{8,10},{9,11},{10,... | collective-permute-start | bytes 393224 | tf_op jit(solution)/shard_map/ppermute | solution.py:24
  3.7 14.7 %collective-permute-start = (bf16[16,4096]{1,0:T(8,128)(2,1)}, bf16[16,4096]{1,0:T(8,128)(2,1)S(1)}, u32[]{:S(2)}, u32[]{:S(2)}) collective-permute-start(bf16[16,4096]{1,0:T(8,128)(2,1)} %param.6), channel_id=1, source_target_pairs={{0,4},{1,5},{2,6},{3,7},{4,0},{5,1},{6,2},{7,3},{8,12},{9,13},{10,... | collective-permute-start | bytes 393224 | tf_op jit(solution)/shard_map/ppermute | solution.py:24
  5.2 12.0 %collective-permute-start.1 = (bf16[16,4096]{1,0:T(8,128)(2,1)}, bf16[16,4096]{1,0:T(8,128)(2,1)S(1)}, u32[]{:S(2)}, u32[]{:S(2)}) collective-permute-start(bf16[16,4096]{1,0:T(8,128)(2,1)} %param.6), channel_id=1, source_target_pairs={{0,8},{1,9},{2,10},{3,11},{4,12},{5,13},{6,14},{7,15},{8,0},{9,1},... | collective-permute-start | bytes 393224 | tf_op jit(solution)/shard_map/ppermute | solution.py:24
  17.3 7.3 %collective-permute-start.9 = (bf16[16,4096]{1,0:T(8,128)(2,1)S(1)}, bf16[16,4096]{1,0:T(8,128)(2,1)S(1)}, u32[]{:S(2)}, u32[]{:S(2)}) collective-permute-start(bf16[16,4096]{1,0:T(8,128)(2,1)S(1)} %collective-permute-done.1), channel_id=1, source_target_pairs={{0,2},{1,3},{2,0},{3,1},{4,6},{5,7},{6,4},{7,5},{8,10},{9,11},{10,... | collective-permute-start | bytes 393224 | tf_op jit(solution)/shard_map/ppermute | solution.py:24
  17.9 5.0 %collective-permute-start.2 = (bf16[16,4096]{1,0:T(8,128)(2,1)S(1)}, bf16[16,4096]{1,0:T(8,128)(2,1)S(1)}, u32[]{:S(2)}, u32[]{:S(2)}) collective-permute-start(bf16[16,4096]{1,0:T(8,128)(2,1)S(1)} %collective-permute-done.1), channel_id=1, source_target_pairs={{0,4},{1,5},{2,6},{3,7},{4,0},{5,1},{6,2},{7,3},{8,12},{9,13},{10,... | collective-permute-start | bytes 393224 | tf_op jit(solution)/shard_map/ppermute | solution.py:24
  18.3 6.2 %collective-permute-start.8 = (bf16[16,4096]{1,0:T(8,128)(2,1)S(1)}, bf16[16,4096]{1,0:T(8,128)(2,1)S(1)}, u32[]{:S(2)}, u32[]{:S(2)}) collective-permute-start(bf16[16,4096]{1,0:T(8,128)(2,1)S(1)} %collective-permute-done), channel_id=1, source_target_pairs={{0,2},{1,3},{2,0},{3,1},{4,6},{5,7},{6,4},{7,5},{8,10},{9,11},{10,... | collective-permute-start | bytes 393224 | tf_op jit(solution)/shard_map/ppermute | solution.py:24
  22.8 6.1 %collective-permute-start.3 = (bf16[64,4096]{1,0:T(8,128)(2,1)S(1)}, bf16[64,4096]{1,0:T(8,128)(2,1)S(1)}, u32[]{:S(2)}, u32[]{:S(2)}) collective-permute-start(bf16[64,4096]{1,0:T(8,128)(2,1)S(1)} %constant_dynamic-update-slice_fusion.x0.refs_0_), channel_id=1, source_target_pairs={{0,1},{1,0},{2,3},{3,2},{4,5},{5,4},{6,7},{7,6},{8,9},{9,8},{10,11... | collective-permute-start | bytes 1572872 | tf_op jit(solution)/shard_map/ppermute | solution.py:24
  22.9 5.9 %collective-permute-start.10 = (bf16[16,4096]{1,0:T(8,128)(2,1)S(1)}, bf16[16,4096]{1,0:T(8,128)(2,1)S(1)}, u32[]{:S(2)}, u32[]{:S(2)}) collective-permute-start(bf16[16,4096]{1,0:T(8,128)(2,1)S(1)} %collective-permute-done.2), channel_id=1, source_target_pairs={{0,2},{1,3},{2,0},{3,1},{4,6},{5,7},{6,4},{7,5},{8,10},{9,11},{10,... | collective-permute-start | bytes 393224 | tf_op jit(solution)/shard_map/ppermute | solution.py:24
  28.8 8.0 %collective-permute-start.11 = (bf16[64,4096]{1,0:T(8,128)(2,1)S(1)}, bf16[64,4096]{1,0:T(8,128)(2,1)S(1)}, u32[]{:S(2)}, u32[]{:S(2)}) collective-permute-start(bf16[64,4096]{1,0:T(8,128)(2,1)S(1)} %constant_dynamic-update-slice_fusion.4.x0.refs_2_), channel_id=1, source_target_pairs={{0,1},{1,0},{2,3},{3,2},{4,5},{5,4},{6,7},{7,6},{8,9},{9,8},{10,11... | collective-permute-start | bytes 1572872 | tf_op jit(solution)/shard_map/ppermute | solution.py:24
  31.3 14.9 %collective-permute-start.4 = (bf16[128,2048]{1,0:T(8,128)(2,1)S(1)}, bf16[128,2048]{1,0:T(8,128)(2,1)S(1)}, u32[]{:S(2)}, u32[]{:S(2)}) collective-permute-start(bf16[128,2048]{1,0:T(8,128)(2,1)S(1)} %get-tuple-element.32), channel_id=1, source_target_pairs={{0,16},{16,0},{1,17},{17,1},{2,18},{18,2},{3,19},{19,3},{4,20},{20... | collective-permute-start | bytes 1572872 | tf_op jit(solution)/shard_map/ppermute | solution.py:29
  39.2 17.7 %collective-permute-start.12 = (bf16[128,2048]{1,0:T(8,128)(2,1)S(1)}, bf16[128,2048]{1,0:T(8,128)(2,1)S(1)}, u32[]{:S(2)}, u32[]{:S(2)}) collective-permute-start(bf16[128,2048]{1,0:T(8,128)(2,1)S(1)} %get-tuple-element.36), channel_id=1, source_target_pairs={{0,16},{16,0},{1,17},{17,1},{2,18},{18,2},{3,19},{19,3},{4,20},{20... | collective-permute-start | bytes 1572872 | tf_op jit(solution)/shard_map/ppermute | solution.py:29
  47.4 10.8 %collective-permute-start.5 = (bf16[64,4096]{1,0:T(8,128)(2,1)S(1)}, bf16[64,4096]{1,0:T(8,128)(2,1)S(1)}, u32[]{:S(2)}, u32[]{:S(2)}) collective-permute-start(bf16[64,4096]{1,0:T(8,128)(2,1)S(1)} %get-tuple-element.34), channel_id=1, source_target_pairs={{0,1},{1,0},{2,3},{3,2},{4,5},{5,4},{6,7},{7,6},{8,9},{9,8},{10,11... | collective-permute-start | bytes 1572872 | tf_op jit(solution)/shard_map/ppermute | solution.py:24
  56.9 22.0 %copy-start = (bf16[16,4096]{1,0:T(8,128)(2,1)S(1)}, bf16[16,4096]{1,0:T(8,128)(2,1)}, u32[]{:S(2)}) copy-start(bf16[16,4096]{1,0:T(8,128)(2,1)} %param.7) | copy-start | bytes 393220
  58.2 2.0 %collective-permute-start.13 = (bf16[64,4096]{1,0:T(8,128)(2,1)S(1)}, bf16[64,4096]{1,0:T(8,128)(2,1)S(1)}, u32[]{:S(2)}, u32[]{:S(2)}) collective-permute-start(bf16[64,4096]{1,0:T(8,128)(2,1)S(1)} %get-tuple-element.38), channel_id=1, source_target_pairs={{0,1},{1,0},{2,3},{3,2},{4,5},{5,4},{6,7},{7,6},{8,9},{9,8},{10,11... | collective-permute-start | bytes 1572872 | tf_op jit(solution)/shard_map/ppermute | solution.py:24
  60.3 6.4 %collective-permute-start.18 = (bf16[16,4096]{1,0:T(8,128)(2,1)S(1)}, bf16[16,4096]{1,0:T(8,128)(2,1)S(1)}, u32[]{:S(2)}, u32[]{:S(2)}) collective-permute-start(bf16[16,4096]{1,0:T(8,128)(2,1)S(1)} %get-tuple-element.64), channel_id=1, source_target_pairs={{0,2},{1,3},{2,0},{3,1},{4,6},{5,7},{6,4},{7,5},{8,10},{9,11},{10,... | collective-permute-start | bytes 393224 | tf_op jit(solution)/shard_map/ppermute | solution.py:24
  61.9 5.3 %collective-permute-start.6 = (bf16[16,4096]{1,0:T(8,128)(2,1)S(1)}, bf16[16,4096]{1,0:T(8,128)(2,1)S(1)}, u32[]{:S(2)}, u32[]{:S(2)}) collective-permute-start(bf16[16,4096]{1,0:T(8,128)(2,1)S(1)} %slice.144), channel_id=1, source_target_pairs={{0,4},{1,5},{2,6},{3,7},{4,0},{5,1},{6,2},{7,3},{8,12},{9,13},{10,... | collective-permute-start | bytes 393224 | tf_op jit(solution)/shard_map/ppermute | solution.py:24
  62.3 10.0 %collective-permute-start.14 = (bf16[16,4096]{1,0:T(8,128)(2,1)S(1)}, bf16[16,4096]{1,0:T(8,128)(2,1)S(1)}, u32[]{:S(2)}, u32[]{:S(2)}) collective-permute-start(bf16[16,4096]{1,0:T(8,128)(2,1)S(1)} %get-tuple-element.66), channel_id=1, source_target_pairs={{0,2},{1,3},{2,0},{3,1},{4,6},{5,7},{6,4},{7,5},{8,10},{9,11},{10,... | collective-permute-start | bytes 393224 | tf_op jit(solution)/shard_map/ppermute | solution.py:24
  62.9 11.5 %collective-permute-start.16 = (bf16[16,4096]{1,0:T(8,128)(2,1)S(1)}, bf16[16,4096]{1,0:T(8,128)(2,1)S(1)}, u32[]{:S(2)}, u32[]{:S(2)}) collective-permute-start(bf16[16,4096]{1,0:T(8,128)(2,1)S(1)} %get-tuple-element.65), channel_id=1, source_target_pairs={{0,2},{1,3},{2,0},{3,1},{4,6},{5,7},{6,4},{7,5},{8,10},{9,11},{10,... | collective-permute-start | bytes 393224 | tf_op jit(solution)/shard_map/ppermute | solution.py:24
  64.4 10.0 %collective-permute-start.15 = (bf16[16,4096]{1,0:T(8,128)(2,1)S(1)}, bf16[16,4096]{1,0:T(8,128)(2,1)S(1)}, u32[]{:S(2)}, u32[]{:S(2)}) collective-permute-start(bf16[16,4096]{1,0:T(8,128)(2,1)S(1)} %get-tuple-element.63), channel_id=1, source_target_pairs={{0,14},{1,15},{2,12},{3,13},{4,10},{5,11},{6,8},{7,9},{8,6},{9,7},... | collective-permute-start | bytes 393224 | tf_op jit(solution)/shard_map/ppermute | solution.py:24
  72.5 6.4 %collective-permute-start.19 = (bf16[16,4096]{1,0:T(8,128)(2,1)S(1)}, bf16[16,4096]{1,0:T(8,128)(2,1)S(1)}, u32[]{:S(2)}, u32[]{:S(2)}) collective-permute-start(bf16[16,4096]{1,0:T(8,128)(2,1)S(1)} %fusion.7), channel_id=1, source_target_pairs={{0,4},{1,5},{2,6},{3,7},{4,0},{5,1},{6,2},{7,3},{8,12},{9,13},{10,... | collective-permute-start | bytes 393224 | tf_op jit(solution)/shard_map/ppermute | solution.py:24
  72.5 6.4 %collective-permute-start.17 = (bf16[16,4096]{1,0:T(8,128)(2,1)S(1)}, bf16[16,4096]{1,0:T(8,128)(2,1)S(1)}, u32[]{:S(2)}, u32[]{:S(2)}) collective-permute-start(bf16[16,4096]{1,0:T(8,128)(2,1)S(1)} %fusion.9.x), channel_id=1, source_target_pairs={{0,8},{1,9},{2,10},{3,11},{4,12},{5,13},{6,14},{7,15},{8,0},{9,1},... | collective-permute-start | bytes 393224 | tf_op jit(solution)/shard_map/ppermute | solution.py:24
  79.7 6.0 %collective-permute-start.21 = (bf16[16,4096]{1,0:T(8,128)(2,1)S(1)}, bf16[16,4096]{1,0:T(8,128)(2,1)S(1)}, u32[]{:S(2)}, u32[]{:S(2)}) collective-permute-start(bf16[16,4096]{1,0:T(8,128)(2,1)S(1)} %get-tuple-element.57), channel_id=1, source_target_pairs={{0,8},{1,9},{2,10},{3,11},{4,12},{5,13},{6,14},{7,15},{8,0},{9,1},... | collective-permute-start | bytes 393224 | tf_op jit(solution)/shard_map/ppermute | solution.py:24
  80.8 8.9 %collective-permute-start.25 = (bf16[16,4096]{1,0:T(8,128)(2,1)S(1)}, bf16[16,4096]{1,0:T(8,128)(2,1)S(1)}, u32[]{:S(2)}, u32[]{:S(2)}) collective-permute-start(bf16[16,4096]{1,0:T(8,128)(2,1)S(1)} %get-tuple-element.57), channel_id=1, source_target_pairs={{0,2},{1,3},{2,0},{3,1},{4,6},{5,7},{6,4},{7,5},{8,10},{9,11},{10,... | collective-permute-start | bytes 393224 | tf_op jit(solution)/shard_map/ppermute | solution.py:24
  82.1 7.6 %collective-permute-start.20 = (bf16[16,4096]{1,0:T(8,128)(2,1)S(1)}, bf16[16,4096]{1,0:T(8,128)(2,1)S(1)}, u32[]{:S(2)}, u32[]{:S(2)}) collective-permute-start(bf16[16,4096]{1,0:T(8,128)(2,1)S(1)} %get-tuple-element.57), channel_id=1, source_target_pairs={{0,4},{1,5},{2,6},{3,7},{4,0},{5,1},{6,2},{7,3},{8,12},{9,13},{10,... | collective-permute-start | bytes 393224 | tf_op jit(solution)/shard_map/ppermute | solution.py:24
  85.6 5.5 %collective-permute-start.22 = (bf16[16,4096]{1,0:T(8,128)(2,1)S(1)}, bf16[16,4096]{1,0:T(8,128)(2,1)S(1)}, u32[]{:S(2)}, u32[]{:S(2)}) collective-permute-start(bf16[16,4096]{1,0:T(8,128)(2,1)S(1)} %collective-permute-done.21.x), channel_id=1, source_target_pairs={{0,4},{1,5},{2,6},{3,7},{4,0},{5,1},{6,2},{7,3},{8,12},{9,13},{10,... | collective-permute-start | bytes 393224 | tf_op jit(solution)/shard_map/ppermute | solution.py:24
  88.1 7.1 %collective-permute-start.27 = (bf16[16,4096]{1,0:T(8,128)(2,1)S(1)}, bf16[16,4096]{1,0:T(8,128)(2,1)S(1)}, u32[]{:S(2)}, u32[]{:S(2)}) collective-permute-start(bf16[16,4096]{1,0:T(8,128)(2,1)S(1)} %collective-permute-done.21.x), channel_id=1, source_target_pairs={{0,2},{1,3},{2,0},{3,1},{4,6},{5,7},{6,4},{7,5},{8,10},{9,11},{10,... | collective-permute-start | bytes 393224 | tf_op jit(solution)/shard_map/ppermute | solution.py:24
  89.7 5.5 %collective-permute-start.26 = (bf16[16,4096]{1,0:T(8,128)(2,1)S(1)}, bf16[16,4096]{1,0:T(8,128)(2,1)S(1)}, u32[]{:S(2)}, u32[]{:S(2)}) collective-permute-start(bf16[16,4096]{1,0:T(8,128)(2,1)S(1)} %collective-permute-done.20.x), channel_id=1, source_target_pairs={{0,2},{1,3},{2,0},{3,1},{4,6},{5,7},{6,4},{7,5},{8,10},{9,11},{10,... | collective-permute-start | bytes 393224 | tf_op jit(solution)/shard_map/ppermute | solution.py:24
  91.1 6.5 %collective-permute-start.23 = (bf16[64,4096]{1,0:T(8,128)(2,1)S(1)}, bf16[64,4096]{1,0:T(8,128)(2,1)S(1)}, u32[]{:S(2)}, u32[]{:S(2)}) collective-permute-start(bf16[64,4096]{1,0:T(8,128)(2,1)S(1)} %pad_maximum_fusion.e0.refs_2_), channel_id=1, source_target_pairs={{0,1},{1,0},{2,3},{3,2},{4,5},{5,4},{6,7},{7,6},{8,9},{9,8},{10,11... | collective-permute-start | bytes 1572872 | tf_op jit(solution)/shard_map/ppermute | solution.py:24
  91.2 6.4 %collective-permute-start.28 = (bf16[16,4096]{1,0:T(8,128)(2,1)S(1)}, bf16[16,4096]{1,0:T(8,128)(2,1)S(1)}, u32[]{:S(2)}, u32[]{:S(2)}) collective-permute-start(bf16[16,4096]{1,0:T(8,128)(2,1)S(1)} %collective-permute-done.22), channel_id=1, source_target_pairs={{0,2},{1,3},{2,0},{3,1},{4,6},{5,7},{6,4},{7,5},{8,10},{9,11},{10,... | collective-permute-start | bytes 393224 | tf_op jit(solution)/shard_map/ppermute | solution.py:24
  97.6 4.1 %collective-permute-start.29 = (bf16[64,4096]{1,0:T(8,128)(2,1)S(1)}, bf16[64,4096]{1,0:T(8,128)(2,1)S(1)}, u32[]{:S(2)}, u32[]{:S(2)}) collective-permute-start(bf16[64,4096]{1,0:T(8,128)(2,1)S(1)} %constant_dynamic-update-slice_fusion.8.e0.refs_4_), channel_id=1, source_target_pairs={{0,1},{1,0},{2,3},{3,2},{4,5},{5,4},{6,7},{7,6},{8,9},{9,8},{10,11... | collective-permute-start | bytes 1572872 | tf_op jit(solution)/shard_map/ppermute | solution.py:24
  100.1 9.2 %collective-permute-start.24 = (bf16[128,1024]{1,0:T(8,128)(2,1)S(1)}, bf16[128,1024]{1,0:T(8,128)(2,1)S(1)}, u32[]{:S(2)}, u32[]{:S(2)}) collective-permute-start(bf16[128,1024]{1,0:T(8,128)(2,1)S(1)} %get-tuple-element.41), channel_id=1, source_target_pairs={{0,16},{16,0},{1,17},{17,1},{2,18},{18,2},{3,19},{19,3},{4,20},{20... | collective-permute-start | bytes 786440 | tf_op jit(solution)/shard_map/ppermute | solution.py:29
  104.1 10.4 %collective-permute-start.30 = (bf16[128,1024]{1,0:T(8,128)(2,1)S(1)}, bf16[128,1024]{1,0:T(8,128)(2,1)S(1)}, u32[]{:S(2)}, u32[]{:S(2)}) collective-permute-start(bf16[128,1024]{1,0:T(8,128)(2,1)S(1)} %get-tuple-element.43), channel_id=1, source_target_pairs={{0,16},{16,0},{1,17},{17,1},{2,18},{18,2},{3,19},{19,3},{4,20},{20... | collective-permute-start | bytes 786440 | tf_op jit(solution)/shard_map/ppermute | solution.py:29
  119.6 10.4 %collective-permute-start.32 = (bf16[64,4096]{1,0:T(8,128)(2,1)S(1)}, bf16[64,4096]{1,0:T(8,128)(2,1)S(1)}, u32[]{:S(2)}, u32[]{:S(2)}) collective-permute-start(bf16[64,4096]{1,0:T(8,128)(2,1)S(1)} %get-tuple-element.47), channel_id=1, source_target_pairs={{0,1},{1,0},{2,3},{3,2},{4,5},{5,4},{6,7},{7,6},{8,9},{9,8},{10,11... | collective-permute-start | bytes 1572872 | tf_op jit(solution)/shard_map/ppermute | solution.py:24
  129.6 2.0 %collective-permute-start.31 = (bf16[64,4096]{1,0:T(8,128)(2,1)S(1)}, bf16[64,4096]{1,0:T(8,128)(2,1)S(1)}, u32[]{:S(2)}, u32[]{:S(2)}) collective-permute-start(bf16[64,4096]{1,0:T(8,128)(2,1)S(1)} %get-tuple-element.45), channel_id=1, source_target_pairs={{0,1},{1,0},{2,3},{3,2},{4,5},{5,4},{6,7},{7,6},{8,9},{9,8},{10,11... | collective-permute-start | bytes 1572872 | tf_op jit(solution)/shard_map/ppermute | solution.py:24
  130.2 15.1 %collective-permute-start.36 = (bf16[16,4096]{1,0:T(8,128)(2,1)S(1)}, bf16[16,4096]{1,0:T(8,128)(2,1)S(1)}, u32[]{:S(2)}, u32[]{:S(2)}) collective-permute-start(bf16[16,4096]{1,0:T(8,128)(2,1)S(1)} %get-tuple-element.61), channel_id=1, source_target_pairs={{0,2},{1,3},{2,0},{3,1},{4,6},{5,7},{6,4},{7,5},{8,10},{9,11},{10,... | collective-permute-start | bytes 393224 | tf_op jit(solution)/shard_map/ppermute | solution.py:24
  131.7 13.6 %collective-permute-start.35 = (bf16[16,4096]{1,0:T(8,128)(2,1)S(1)}, bf16[16,4096]{1,0:T(8,128)(2,1)S(1)}, u32[]{:S(2)}, u32[]{:S(2)}) collective-permute-start(bf16[16,4096]{1,0:T(8,128)(2,1)S(1)} %slice.143), channel_id=1, source_target_pairs={{0,4},{1,5},{2,6},{3,7},{4,0},{5,1},{6,2},{7,3},{8,12},{9,13},{10,... | collective-permute-start | bytes 393224 | tf_op jit(solution)/shard_map/ppermute | solution.py:24
  141.0 6.4 %collective-permute-start.38 = (bf16[16,4096]{1,0:T(8,128)(2,1)S(1)}, bf16[16,4096]{1,0:T(8,128)(2,1)S(1)}, u32[]{:S(2)}, u32[]{:S(2)}) collective-permute-start(bf16[16,4096]{1,0:T(8,128)(2,1)S(1)} %get-tuple-element.60), channel_id=1, source_target_pairs={{0,2},{1,3},{2,0},{3,1},{4,6},{5,7},{6,4},{7,5},{8,10},{9,11},{10,... | collective-permute-start | bytes 393224 | tf_op jit(solution)/shard_map/ppermute | solution.py:24
  142.3 14.5 %collective-permute-start.34 = (bf16[16,4096]{1,0:T(8,128)(2,1)S(1)}, bf16[16,4096]{1,0:T(8,128)(2,1)S(1)}, u32[]{:S(2)}, u32[]{:S(2)}) collective-permute-start(bf16[16,4096]{1,0:T(8,128)(2,1)S(1)} %get-tuple-element.62), channel_id=1, source_target_pairs={{0,2},{1,3},{2,0},{3,1},{4,6},{5,7},{6,4},{7,5},{8,10},{9,11},{10,... | collective-permute-start | bytes 393224 | tf_op jit(solution)/shard_map/ppermute | solution.py:24
  143.0 13.8 %collective-permute-start.33 = (bf16[16,4096]{1,0:T(8,128)(2,1)S(1)}, bf16[16,4096]{1,0:T(8,128)(2,1)S(1)}, u32[]{:S(2)}, u32[]{:S(2)}) collective-permute-start(bf16[16,4096]{1,0:T(8,128)(2,1)S(1)} %get-tuple-element.59), channel_id=1, source_target_pairs={{0,14},{1,15},{2,12},{3,13},{4,10},{5,11},{6,8},{7,9},{8,6},{9,7},... | collective-permute-start | bytes 393224 | tf_op jit(solution)/shard_map/ppermute | solution.py:24
  145.4 11.6 %collective-permute-start.37 = (bf16[16,4096]{1,0:T(8,128)(2,1)S(1)}, bf16[16,4096]{1,0:T(8,128)(2,1)S(1)}, u32[]{:S(2)}, u32[]{:S(2)}) collective-permute-start(bf16[16,4096]{1,0:T(8,128)(2,1)S(1)} %fusion.2), channel_id=1, source_target_pairs={{0,8},{1,9},{2,10},{3,11},{4,12},{5,13},{6,14},{7,15},{8,0},{9,1},... | collective-permute-start | bytes 393224 | tf_op jit(solution)/shard_map/ppermute | solution.py:24
  147.4 9.4 %collective-permute-start.39 = (bf16[16,4096]{1,0:T(8,128)(2,1)S(1)}, bf16[16,4096]{1,0:T(8,128)(2,1)S(1)}, u32[]{:S(2)}, u32[]{:S(2)}) collective-permute-start(bf16[16,4096]{1,0:T(8,128)(2,1)S(1)} %fusion), channel_id=1, source_target_pairs={{0,4},{1,5},{2,6},{3,7},{4,0},{5,1},{6,2},{7,3},{8,12},{9,13},{10,... | collective-permute-start | bytes 393224 | tf_op jit(solution)/shard_map/ppermute | solution.py:24
